TPU v7x, 32 devices: a whole 2x2x4 slice. The times are simulated.
32 devices in a mesh: ctx: 8 (over z, y), wa: 4 (over x, core).
Axes of the slice: x: 2, y: 2, z: 4, core: 2. Of those that a mesh axis runs over, the one named last changes fastest.
Arguments:
- layer_input: bfloat16 [16, 2048, 768], P('wa', 'ctx'), may hold values from -6 to 6
- cotangent: bfloat16 [16, 2048, 768], P('wa', 'ctx'), may hold values from -12 to 12
- attention_gain: float32 [768], replicated, may hold values from 0.5 to 1.5
- qkv_proj: bfloat16 [768, 2304], P(None, 'wa'), may hold values from -0.21875 to 0.21875
- out_proj: bfloat16 [768, 768], P('wa'), may hold values from -0.875 to 0.875
- feed_gain: float32 [768], replicated, may hold values from 0.5 to 1.5
- in_proj: bfloat16 [768, 2304], P(None, 'wa'), may hold values from -0.21875 to 0.21875
- down_proj: bfloat16 [1152, 768], P('wa'), may hold values from -0.25 to 0.25
Outputs:
- output: bfloat16 [16, 2048, 768], P('wa', 'ctx')
- input_grad: float32 [16, 2048, 768], P('wa', 'ctx')
- attention_gain_grad: float32 [768], replicated
- feed_gain_grad: float32 [768], replicated
- qkv_proj_grad: float32 [768, 2304], P(None, 'wa')
- out_proj_grad: float32 [768, 768], P('wa')
- in_proj_grad: float32 [768, 2304], P(None, 'wa')
- down_proj_grad: float32 [1152, 768], P('wa')
All inputs are finite; a program needn't handle non-finite values.
Results may differ from a plain program's by a relative error of at most 0.018.
Values may be sent and summed in bfloat16 or wider, within the bound.
No kernel may reach another device: no remote copies, remote signals or barrier semaphores. Data moves between devices by JAX's collectives and lax.ppermute only.
A program may use at most 192 MiB of HBM per device.

v0:
```python
import math

import jax
import jax.numpy as jnp
from jax import lax
from jax.sharding import PartitionSpec as P

HEAD = 64
FF = 1152
HALF = 64


def padded(cells, sides, width):
    for axis, dim in sides:
        count = lax.axis_size(axis)
        ends = count - 1
        head = lax.slice_in_dim(cells, 0, width, axis=dim)
        tail = lax.slice_in_dim(cells, cells.shape[dim] - width, cells.shape[dim], axis=dim)
        cells = jnp.concatenate(
            [
                lax.ppermute(tail, axis, [(i, (i + 1) % count) for i in range(ends)]),
                cells,
                lax.ppermute(head, axis, [((i + 1) % count, i) for i in range(ends)]),
            ],
            axis=dim,
        )
    return cells


def layer_stats(values):
    center = values - jnp.mean(values, -1, keepdims=True)
    spread = jnp.mean(center * center, -1, keepdims=True)
    inverse = lax.rsqrt(spread + 1e-05)
    return (center * inverse, inverse)


def norm_back(grad_out, gain, normal, inverse):
    scaled = grad_out * gain
    gain_grad = jnp.sum(grad_out * normal, 0)
    input_part = inverse * (
        scaled
        - jnp.mean(scaled, -1, keepdims=True)
        - normal * jnp.mean(scaled * normal, -1, keepdims=True)
    )
    return (input_part, gain_grad)


def rotary_tables(places):
    frequencies = jnp.power(10000.0, -jnp.arange(0, HEAD, 2, dtype=jnp.float32) / HEAD)
    angles = places.astype(jnp.float32)[:, None] * frequencies[None, :]
    cosine = jnp.concatenate([jnp.cos(angles), jnp.cos(angles)], -1)
    sine = jnp.concatenate([jnp.sin(angles), jnp.sin(angles)], -1)
    return (cosine[None, :, None, :], sine[None, :, None, :])


def rotate(values, cosine, sine):
    half_len = HEAD // 2
    turned = jnp.concatenate([-values[..., half_len:], values[..., :half_len]], -1)
    return values * cosine + turned * sine


def rotate_back(grads, cosine, sine):
    half_len = HEAD // 2
    sined = grads * sine
    turned = jnp.concatenate([sined[..., half_len:], -sined[..., :half_len]], -1)
    return grads * cosine + turned


def local(
    layer_input, cotangent, attention_gain, qkv_proj, out_proj, feed_gain, in_proj, down_proj
):
    seqs_here, block_len, model_width = layer_input.shape
    heads_count = model_width // HEAD
    rows_here = seqs_here * block_len
    key_span = block_len + 2 * HALF
    scale_factor = HEAD ** (-0.5)
    qkv_weight, out_weight, in_weight, down_weight = (
        lax.all_gather(qkv_proj, "wa", axis=1, tiled=True),
        lax.all_gather(out_proj, "wa", axis=0, tiled=True),
        lax.all_gather(in_proj, "wa", axis=1, tiled=True),
        lax.all_gather(down_proj, "wa", axis=0, tiled=True),
    )
    context_rank = lax.axis_index("ctx")
    seq_len = block_len * lax.axis_size("ctx")
    places = context_rank * block_len + jnp.arange(block_len, dtype=jnp.int32)
    cosine, sine = rotary_tables(places)
    head_shape = (seqs_here, block_len, heads_count, HEAD)
    wide_shape = (seqs_here, key_span, heads_count, HEAD)
    tokens = layer_input.astype(jnp.float32).reshape(rows_here, model_width)
    normal1, inverse1 = layer_stats(tokens)
    normed1 = (normal1 * attention_gain).astype(jnp.bfloat16)
    projected = jnp.dot(normed1, qkv_weight, preferred_element_type=jnp.float32)
    queries = rotate(projected[:, :model_width].reshape(head_shape), cosine, sine).astype(
        jnp.bfloat16
    )
    keys_here = rotate(
        projected[:, model_width : 2 * model_width].reshape(head_shape), cosine, sine
    ).astype(jnp.bfloat16)
    values_here = projected[:, 2 * model_width :].astype(jnp.bfloat16)
    kv_pairs = jnp.concatenate(
        [
            keys_here.reshape(seqs_here, block_len, model_width),
            values_here.reshape(seqs_here, block_len, model_width),
        ],
        -1,
    )
    widened = padded(kv_pairs, (("ctx", 1),), HALF)
    keys_wide = widened[..., :model_width].reshape(wide_shape)
    values_wide = widened[..., model_width:].reshape(wide_shape)
    query_index = jnp.arange(block_len, dtype=jnp.int32)
    key_index = jnp.arange(key_span, dtype=jnp.int32)
    key_place = context_rank * block_len - HALF + key_index
    allowed = (jnp.abs(key_index[None, :] - HALF - query_index[:, None]) <= HALF) & (
        (key_place >= 0) & (key_place < seq_len)
    )[None, :]

    def masked_scores():
        raw_scores = (
            jnp.einsum("sqhd,skhd->shqk", queries, keys_wide, preferred_element_type=jnp.float32)
            * scale_factor
        )
        return jnp.where(allowed[None, None], raw_scores, -1e30)

    masked = masked_scores()
    top_score = jnp.max(masked, -1, keepdims=True)
    exponents = jnp.exp(masked - top_score)
    row_total = jnp.sum(exponents, -1, keepdims=True)
    softmaxed = exponents / row_total
    log_total = top_score + jnp.log(row_total)
    attended = jnp.einsum(
        "shqk,skhd->sqhd",
        softmaxed.astype(jnp.bfloat16),
        values_wide,
        preferred_element_type=jnp.float32,
    )
    attended = attended.reshape(rows_here, model_width).astype(jnp.bfloat16)
    hidden1 = tokens + jnp.dot(attended, out_weight, preferred_element_type=jnp.float32)
    normal2, inverse2 = layer_stats(hidden1)
    normed2 = (normal2 * feed_gain).astype(jnp.bfloat16)
    inner = jnp.dot(normed2, in_weight, preferred_element_type=jnp.float32)
    first_half = inner[:, :FF]
    second_half = inner[:, FF:]
    activated = jax.nn.gelu(first_half, approximate=False)
    mixed = (activated * second_half).astype(jnp.bfloat16)
    output = (
        (hidden1 + jnp.dot(mixed, down_weight, preferred_element_type=jnp.float32))
        .astype(jnp.bfloat16)
        .reshape(layer_input.shape)
    )
    grad_out = cotangent.astype(jnp.float32).reshape(rows_here, model_width)
    grad_low = grad_out.astype(jnp.bfloat16)
    down_grad = jnp.einsum("tf,td->fd", mixed, grad_low, preferred_element_type=jnp.float32)
    mixed_grad = jnp.einsum("td,fd->tf", grad_low, down_weight, preferred_element_type=jnp.float32)
    slope = 0.5 * (1.0 + lax.erf(first_half / math.sqrt(2.0))) + first_half * jnp.exp(
        -0.5 * first_half * first_half
    ) / math.sqrt(2.0 * math.pi)
    inner_grad = jnp.concatenate(
        [mixed_grad * second_half * slope, mixed_grad * activated], -1
    ).astype(jnp.bfloat16)
    in_grad = jnp.einsum("td,tf->df", normed2, inner_grad, preferred_element_type=jnp.float32)
    normed2_grad = jnp.einsum(
        "tf,df->td", inner_grad, in_weight, preferred_element_type=jnp.float32
    )
    hidden_part, second_gain_grad = norm_back(normed2_grad, feed_gain, normal2, inverse2)
    hidden1_grad = grad_out + hidden_part
    branch_grad = hidden1_grad.astype(jnp.bfloat16)
    out_grad = jnp.einsum("te,td->ed", attended, branch_grad, preferred_element_type=jnp.float32)
    attended_grad = (
        jnp.einsum("td,ed->te", branch_grad, out_weight, preferred_element_type=jnp.float32)
        .astype(jnp.bfloat16)
        .reshape(head_shape)
    )
    softmaxed_again = jnp.exp(masked_scores() - log_total)
    softmaxed_grad = jnp.einsum(
        "sqhd,skhd->shqk", attended_grad, values_wide, preferred_element_type=jnp.float32
    )
    score_grad = (
        softmaxed_again
        * (softmaxed_grad - jnp.sum(softmaxed_again * softmaxed_grad, -1, keepdims=True))
    ).astype(jnp.bfloat16)
    query_grad = (
        jnp.einsum("shqk,skhd->sqhd", score_grad, keys_wide, preferred_element_type=jnp.float32)
        * scale_factor
    )
    key_grad = (
        jnp.einsum("shqk,sqhd->skhd", score_grad, queries, preferred_element_type=jnp.float32)
        * scale_factor
    )
    value_grad = jnp.einsum(
        "shqk,sqhd->skhd",
        softmaxed_again.astype(jnp.bfloat16),
        attended_grad,
        preferred_element_type=jnp.float32,
    )
    pair_grad = jnp.concatenate(
        [
            key_grad.reshape(seqs_here, key_span, model_width),
            value_grad.reshape(seqs_here, key_span, model_width),
        ],
        -1,
    )
    edge_rows = jnp.concatenate([pair_grad[:, :HALF], pair_grad[:, block_len + HALF :]], 1)
    returned = padded(edge_rows.astype(jnp.bfloat16), (("ctx", 1),), HALF).astype(edge_rows.dtype)
    own_grad = pair_grad[:, HALF : HALF + block_len]
    own_grad = own_grad.at[:, :HALF].add(returned[:, :HALF])
    own_grad = own_grad.at[:, block_len - HALF :].add(returned[:, 3 * HALF :])
    keys_back = rotate_back(own_grad[..., :model_width].reshape(head_shape), cosine, sine)
    queries_back = rotate_back(query_grad, cosine, sine)
    projected_grad = jnp.concatenate(
        [
            queries_back.reshape(rows_here, model_width),
            keys_back.reshape(rows_here, model_width),
            own_grad[..., model_width:].reshape(rows_here, model_width),
        ],
        -1,
    ).astype(jnp.bfloat16)
    qkv_weight_grad = jnp.einsum(
        "td,tf->df", normed1, projected_grad, preferred_element_type=jnp.float32
    )
    normed1_grad = jnp.einsum(
        "tf,df->td", projected_grad, qkv_weight, preferred_element_type=jnp.float32
    )
    token_part, first_gain_grad = norm_back(normed1_grad, attention_gain, normal1, inverse1)
    input_grad = (hidden1_grad + token_part).reshape(layer_input.shape)
    first_gain_total, second_gain_total = lax.psum(
        (first_gain_grad, second_gain_grad), ("ctx", "wa")
    )
    summed = lax.psum((qkv_weight_grad, out_grad, in_grad, down_grad), "ctx")
    shards = (
        lax.psum_scatter(
            summed[0].astype(jnp.bfloat16), "wa", scatter_dimension=1, tiled=True
        ).astype(jnp.float32),
        lax.psum_scatter(
            summed[1].astype(jnp.bfloat16), "wa", scatter_dimension=0, tiled=True
        ).astype(jnp.float32),
        lax.psum_scatter(
            summed[2].astype(jnp.bfloat16), "wa", scatter_dimension=1, tiled=True
        ).astype(jnp.float32),
        lax.psum_scatter(
            summed[3].astype(jnp.bfloat16), "wa", scatter_dimension=0, tiled=True
        ).astype(jnp.float32),
    )
    return (
        output,
        input_grad,
        first_gain_total,
        second_gain_total,
        shards[0],
        shards[1],
        shards[2],
        shards[3],
    )


def solution(mesh):
    return jax.shard_map(
        local,
        mesh=mesh,
        in_specs=(
            P("wa", "ctx", None),
            P("wa", "ctx", None),
            P(),
            P(None, "wa"),
            P("wa", None),
            P(),
            P(None, "wa"),
            P("wa", None),
        ),
        out_specs=(
            P("wa", "ctx", None),
            P("wa", "ctx", None),
            P(),
            P(),
            P(None, "wa"),
            P("wa", None),
            P(None, "wa"),
            P("wa", None),
        ),
        check_vma=False,
    )
```

profile of v0, /device:TPU:0, one launch (start us, length us, event | category | flops | bytes accessed | tf_op | source)
XLA Modules:
  0.0 1267.3 jit_solution(1546155793572672629)
XLA Ops:
  12.5 30.6 %all-gather.5.cloned.1.call-done = bf16[768,2304]{0,1:T(8,128)(2,1)} async-done(((bf16[768,576]{0,1:T(8,128)(2,1)}), bf16[768,2304]{0,1:T(8,128)(2,1)}) %all-gather.5.cloned.1.call-update) | async-done | bytes 3538960 | tf_op jit(solution)/shard_map/all_gather | solution.py:78
  43.1 5.9 fusion.83
  103.1 14.3 %collective-permute-done = bf16[4,64,1536]{2,1,0:T(8,128)(2,1)} collective-permute-done((bf16[4,64,1536]{2,1,0:T(8,128)(2,1)}, bf16[4,64,1536]{2,1,0:T(8,128)(2,1)}, u32[]{:S(2)}, u32[]{:S(2)}) %collective-permute-start) | collective-permute-done | bytes 786464 | tf_op jit(solution)/shard_map/ppermute | solution.py:21
  127.5 5.8 fusion.7
  133.3 5.5 fusion
  140.4 7.6 fusion.52
  155.4 10.7 fusion.75
  166.0 17.7 %multiply_convert_fusion.1 = (bf16[1024,1152]{1,0:T(8,128)(2,1)S(1)}, f32[1024,1152]{1,0:T(8,128)}, bf16[1024,1152]{1,0:T(8,128)(2,1)S(1)}) fusion(f32[1024,2304]{1,0:T(8,128)} %fusion.75, bf16[1024,768]{1,0:T(8,128)(2,1)S(1)} %bitcast.139, bf16[1152,768]{1,0:T(8,128)(2,1)} %all-gather.11.cloned.1.call-done), kind=kOutput, calls=%fused_computation.32 | convolution fusion | flops 1902772224 | bytes 22216704 | tf_op jit(solution)/shard_map/td,fd->tf/dot_general | solution.py:153
  200.5 14.7 %multiply_reduce_fusion = (f32[4,12,256]{2,1,0:T(8,128)S(1)}, f32[4,12,256,384]{3,2,1,0:T(8,128)}) fusion(f32[4,12,256]{2,1,0:T(8,128)S(1)} %log_add_fusion, f32[4,12,256,384]{3,2,1,0:T(8,128)} %copy-done, pred[256,384]{1,0:T(8,128)(4,1)S(1)} %fusion.62, bf16[4,384,12,64]{1,3,2,0:T(8,128)(2,1)S(1)} %bitcast.123, bf16[4,256,12,64]{1,0,3,2:T(4,128)(2,1)} %reshape.287), kind=kOutput, calls=%fused_computation.1 | convolution fusion | flops 627560448 | bytes 41877504 | tf_op jit(solution)/shard_map/sqhd,skhd->shqk/dot_general | solution.py:174
  215.2 10.5 fusion.3
  228.9 9.5 fusion.42
  243.1 10.1 multiply_convert_fusion
  258.2 6.1 copy.58
  264.3 6.1 copy.59
  276.3 5.5 collective-permute-start.2
  281.8 6.8 bitcast_multiply_fusion
  298.0 16.1 %collective-permute-done.2 = bf16[4,64,1536]{2,1,0:T(8,128)(2,1)S(1)} collective-permute-done((bf16[4,64,1536]{2,1,0:T(8,128)(2,1)S(1)}, bf16[4,64,1536]{2,1,0:T(8,128)(2,1)S(1)}, u32[]{:S(2)}, u32[]{:S(2)}) %collective-permute-start.2) | collective-permute-done | bytes 786464 | tf_op jit(solution)/shard_map/ppermute | solution.py:21
  336.4 9.2 fusion.44
  345.6 768.2 %all-reduce.3 = (bf16[768,2304]{0,1:T(8,128)(2,1)}, bf16[768,768]{1,0:T(8,128)(2,1)}, bf16[768,2304]{0,1:T(8,128)(2,1)}, bf16[1152,768]{1,0:T(8,128)(2,1)}) all-reduce(f32[768,2304]{0,1:T(8,128)} %fusion.44, f32[768,768]{1,0:T(8,128)} %fusion.59, f32[768,2304]{0,1:T(8,128)} %fusion.42, ...), channel_id=1, replica_groups=mesh['ctx'=8,'wa'=4] {'ctx'}, use_global_device_ids=true, to_apply=%region_15.16 | all-reduce | flops 5013504 | bytes 30081024 | tf_op jit(solution)/shard_map/psum | solution.py:228
  1116.0 6.3 add_convert_fusion.1
  1122.4 6.4 fusion.41
  1128.8 39.2 %all-reduce = (f32[768]{0:T(1024)}, f32[768]{0:T(1024)}) all-reduce(f32[768]{0:T(1024)S(1)} %get-tuple-element.34, f32[768]{0:T(1024)S(1)} %get-tuple-element.32), channel_id=1, replica_groups=mesh['ctx'=8,'wa'=4] {'ctx','wa'}, use_global_device_ids=true, to_apply=%region_12.13 | all-reduce | flops 1536 | bytes 12288 | tf_op jit(solution)/shard_map/psum | solution.py:225
  1176.3 38.4 %reduce-scatter.5.cloned.1.call-done = bf16[768,576]{0,1:T(8,128)(2,1)} async-done(((bf16[768,2304]{0,1:T(8,128)(2,1)}), bf16[768,576]{0,1:T(8,128)(2,1)}) %reduce-scatter.5.cloned.1.call-update) | async-done | bytes 884752 | tf_op jit(solution)/shard_map/reduce_scatter | solution.py:230
  1217.3 40.5 %reduce-scatter.9.cloned.1.call-done = bf16[768,576]{0,1:T(8,128)(2,1)} async-done(((bf16[768,2304]{0,1:T(8,128)(2,1)}), bf16[768,576]{0,1:T(8,128)(2,1)}) %reduce-scatter.9.cloned.1.call-update) | async-done | bytes 884752 | tf_op jit(solution)/shard_map/reduce_scatter | solution.py:236
  (241 shorter events, 160.4 us)
Async XLA Ops:
  7.2 35.9 %all-gather.5.cloned.1.call-start = ((), (), s32[]{:S(2)}) async-start(), calls=%async_computation.4 | async-start | bytes 4423680 | tf_op jit(solution)/shard_map/all_gather | solution.py:78
  7.9 141.7 %all-gather.7.cloned.1.call-start = ((), (), s32[]{:S(2)}) async-start(), calls=%async_computation.5 | async-start | bytes 1474560 | tf_op jit(solution)/shard_map/all_gather | solution.py:79
  8.7 146.7 %all-gather.9.cloned.1.call-start = ((), (), s32[]{:S(2)}) async-start(), calls=%async_computation.6 | async-start | bytes 4423680 | tf_op jit(solution)/shard_map/all_gather | solution.py:80
  9.4 156.6 %all-gather.11.cloned.1.call-start = ((), (), s32[]{:S(2)}) async-start(), calls=%async_computation.7 | async-start | bytes 2211840 | tf_op jit(solution)/shard_map/all_gather | solution.py:81
  10.0 1162.6 %reduce-scatter.7.cloned.1.call-start = ((), (), s32[]{:S(2)}) async-start(), calls=%async_computation.9 | async-start | bytes 1474560 | tf_op jit(solution)/shard_map/reduce_scatter | solution.py:233
  11.0 38.0 %copy-start.39 = (f32[1,2,4,128]{3,1,2,0:T(2,128)}, f32[1,2,4,128]{3,1,2,0:T(2,128)S(1)}, u32[]{:S(2)}) copy-start(f32[1,2,4,128]{3,1,2,0:T(2,128)S(1)} %copy.64) | copy-start | bytes 12292
  11.0 37.9 %copy-start.41 = (f32[1,2,4,128]{3,1,2,0:T(2,128)}, f32[1,2,4,128]{3,1,2,0:T(2,128)S(1)}, u32[]{:S(2)}) copy-start(f32[1,2,4,128]{3,1,2,0:T(2,128)S(1)} %copy.63) | copy-start | bytes 12292
  11.9 84.7 %copy-start.35 = (f32[256,64]{0,1:T(8,128)}, f32[256,64]{0,1:T(8,128)S(1)}, u32[]{:S(2)}) copy-start(f32[256,64]{0,1:T(8,128)S(1)} %get-tuple-element.66) | copy-start | bytes 196612
  12.5 30.6 %copy-start.25 = (bf16[1024,768]{1,0:T(8,128)(2,1)}, bf16[1024,768]{1,0:T(8,128)(2,1)S(1)}, u32[]{:S(2)}) copy-start(bf16[1024,768]{1,0:T(8,128)(2,1)S(1)} %fusion.36) | copy-start | bytes 4718596
  78.7 21.9 %collective-permute-start.1 = (bf16[4,64,1536]{2,1,0:T(8,128)(2,1)}, bf16[4,64,1536]{2,1,0:T(8,128)(2,1)}, u32[]{:S(2)}, u32[]{:S(2)}) collective-permute-start(bf16[4,64,1536]{2,1,0:T(8,128)(2,1)} %copy.47), channel_id=1, source_target_pairs={{4,0},{8,4},{12,8},{16,12},{20,16},{24,20},{28,24},{5,1},{9,5},{13... | collective-permute-start | bytes 2359304 | tf_op jit(solution)/shard_map/ppermute | solution.py:23
  81.5 35.9 %collective-permute-start = (bf16[4,64,1536]{2,1,0:T(8,128)(2,1)}, bf16[4,64,1536]{2,1,0:T(8,128)(2,1)}, u32[]{:S(2)}, u32[]{:S(2)}) collective-permute-start(bf16[4,64,1536]{2,1,0:T(8,128)(2,1)} %copy.46), channel_id=1, source_target_pairs={{0,4},{4,8},{8,12},{12,16},{16,20},{20,24},{24,28},{1,5},{5,9},{9,... | collective-permute-start | bytes 2359304 | tf_op jit(solution)/shard_map/ppermute | solution.py:21
  98.9 21.0 %copy-start.9 = (bf16[4,256,768]{1,2,0:T(8,128)(2,1)S(1)}, bf16[4,256,768]{1,2,0:T(8,128)(2,1)}, u32[]{:S(2)}) copy-start(bf16[4,256,768]{1,2,0:T(8,128)(2,1)} %copy-done.8) | copy-start | bytes 4718596
  98.9 21.0 %copy-start.11 = (bf16[4,256,768]{1,2,0:T(8,128)(2,1)S(1)}, bf16[4,256,768]{1,2,0:T(8,128)(2,1)}, u32[]{:S(2)}) copy-start(bf16[4,256,768]{1,2,0:T(8,128)(2,1)} %copy-done.10) | copy-start | bytes 4718596
  166.0 17.8 %copy-start.15 = (f32[1024,768]{1,0:T(8,128)S(1)}, f32[1024,768]{1,0:T(8,128)}, u32[]{:S(2)}) copy-start(f32[1024,768]{1,0:T(8,128)} %copy-done.14) | copy-start | bytes 9437188
  166.0 17.8 %copy-start.47 = (bf16[768,2304]{0,1:T(8,128)(2,1)S(1)}, bf16[768,2304]{0,1:T(8,128)(2,1)}, u32[]{:S(2)}) copy-start(bf16[768,2304]{0,1:T(8,128)(2,1)} %all-gather.9.cloned.1.call-done) | copy-start | bytes 10616836
  200.5 14.7 %copy-start.20 = (bf16[4,256,12,64]{1,0,3,2:T(4,128)(2,1)S(1)}, bf16[4,256,12,64]{1,0,3,2:T(4,128)(2,1)}, u32[]{:S(2)}) copy-start(bf16[4,256,12,64]{1,0,3,2:T(4,128)(2,1)} %reshape.287) | copy-start | bytes 4718596
  228.8 14.2 %slice-start.1 = ((s8[18874368]{0:T(1024)(128)(4,1)}), s8[4194304]{0:T(1024)(128)(4,1)S(1)}, s32[]{:S(2)}) async-start(s8[18874368]{0:T(1024)(128)(4,1)} %bitcast.111), calls=%async_computation.13 | async-start | bytes 8388608
  228.8 14.2 %slice-start.2 = ((s8[18874368]{0:T(1024)(128)(4,1)}), s8[4194304]{0:T(1024)(128)(4,1)S(1)}, s32[]{:S(2)}) async-start(s8[18874368]{0:T(1024)(128)(4,1)} %bitcast.111), calls=%async_computation.14 | async-start | bytes 8388608
  228.8 14.2 %slice-start.3 = ((s8[18874368]{0:T(1024)(128)(4,1)}), s8[2097152]{0:T(1024)(128)(4,1)S(1)}, s32[]{:S(2)}) async-start(s8[18874368]{0:T(1024)(128)(4,1)} %bitcast.111), calls=%async_computation.15 | async-start | bytes 4194304
  274.8 23.1 %collective-permute-start.3 = (bf16[4,64,1536]{2,1,0:T(8,128)(2,1)S(1)}, bf16[4,64,1536]{2,1,0:T(8,128)(2,1)S(1)}, u32[]{:S(2)}, u32[]{:S(2)}) collective-permute-start(bf16[4,64,1536]{2,1,0:T(8,128)(2,1)S(1)} %get-tuple-element.50), channel_id=1, source_target_pairs={{4,0},{8,4},{12,8},{16,12},{20,16},{24,20},{28,24},{5,1},{9,5},{13... | collective-permute-start | bytes 2359304 | tf_op jit(solution)/shard_map/ppermute | solution.py:23
  276.3 37.8 %collective-permute-start.2 = (bf16[4,64,1536]{2,1,0:T(8,128)(2,1)S(1)}, bf16[4,64,1536]{2,1,0:T(8,128)(2,1)S(1)}, u32[]{:S(2)}, u32[]{:S(2)}) collective-permute-start(bf16[4,64,1536]{2,1,0:T(8,128)(2,1)S(1)} %get-tuple-element.49), channel_id=1, source_target_pairs={{0,4},{4,8},{8,12},{12,16},{16,20},{20,24},{24,28},{1,5},{5,9},{9,... | collective-permute-start | bytes 2359304 | tf_op jit(solution)/shard_map/ppermute | solution.py:21
  1113.8 60.5 %reduce-scatter.11.cloned.1.call-start = ((), (), s32[]{:S(2)}) async-start(), calls=%async_computation.11 | async-start | bytes 2211840 | tf_op jit(solution)/shard_map/reduce_scatter | solution.py:239
  1114.4 100.4 %reduce-scatter.5.cloned.1.call-start = ((), (), s32[]{:S(2)}) async-start(), calls=%async_computation.8 | async-start | bytes 4423680 | tf_op jit(solution)/shard_map/reduce_scatter | solution.py:230
  1115.1 142.6 %reduce-scatter.9.cloned.1.call-start = ((), (), s32[]{:S(2)}) async-start(), calls=%async_computation.10 | async-start | bytes 4423680 | tf_op jit(solution)/shard_map/reduce_scatter | solution.py:236
  (52 other events, 279.4 us)
Sparse Core Ops, SparseCore 0:
  9.6 33.4 all-gather.4
  44.6 17.4 all-gather.6
  63.6 30.7 all-gather.8
  95.8 20.7 all-gather.10
  1113.9 24.9 reduce-scatter.6
  1142.0 29.7 reduce-scatter.10
  1174.4 40.3 reduce-scatter.4
  1217.3 40.3 reduce-scatter.8
where the time goes:
time: 1280 us; the launch traced here: 1270 us
  blocking collectives  807 us (63%)
  waiting for transfers between devices  146 us (11%)
  matrix products  132 us (10%)
  local copies, waits for them, and re-layouts  80.6 us (6%)
  other arithmetic  71.7 us (6%)
  between operations  15.4 us (1%)
  starting transfers between devices  13.9 us (1%)
    psum x1, blocking collectives, local(): summed = lax.psum((qkv_weight_grad, out_grad, in_grad, down_grad), 'ctx')  768 us
    reduce_scatter x1, waiting for transfers between devices, local(): lax.psum_scatter(summed[2].astype(jnp.bfloat16), 'wa', scatter_dimension=...  40.5 us
    psum x1, blocking collectives, local(): lax.psum((first_gain_grad, second_gain_grad), ('ctx', 'wa'))  39.2 us
    reduce_scatter x1, waiting for transfers between devices, local(): lax.psum_scatter(summed[0].astype(jnp.bfloat16), 'wa', scatter_dimension=...  38.4 us
    all_gather x1, waiting for transfers between devices, local(): lax.all_gather(qkv_proj, 'wa', axis=1, tiled=True)  30.6 us
    ppermute x2, waiting for transfers between devices, padded(): lax.ppermute(tail, axis, [(i, (i + 1) % count) for i in range(ends)])  30.4 us
  transfers between devices with their start and end apart: 12, of which 6 were waited for; matrix products, arithmetic and copies ran while one was open for 11% of the time, Pallas kernels for 0%

commit v1 on v0

v1 whole, which is shorter than its diff:
```python
import functools
import math

import jax
import jax.numpy as jnp
from jax import lax
from jax.experimental import pallas as pl
from jax.experimental.pallas import tpu as pltpu
from jax.sharding import PartitionSpec as P

HEAD = 64
HALF = 64
QB = 128
LANES = 128
BF = jnp.bfloat16
F32 = jnp.float32
VMEM_LIMIT = 60 * 1024 * 1024
ANY = pl.BlockSpec(memory_space=pl.ANY)


def nn(a, b):
    return lax.dot_general(a, b, (((1,), (0,)), ((), ())), preferred_element_type=F32)


def nt(a, b):
    return lax.dot_general(a, b, (((1,), (1,)), ((), ())), preferred_element_type=F32)


def tn(a, b):
    return lax.dot_general(a, b, (((0,), (0,)), ((), ())), preferred_element_type=F32)


def params(n=1):
    return pltpu.CompilerParams(
        dimension_semantics=("arbitrary",) * n, vmem_limit_bytes=VMEM_LIMIT
    )


def cost(flops, nbytes, trans=0):
    return pl.CostEstimate(
        flops=int(flops), bytes_accessed=int(nbytes), transcendentals=int(trans)
    )


def fetch(rank, parts, full, sems):
    rows = parts[0].shape[0]
    copies = [
        pltpu.make_async_copy(
            part,
            full.at[pl.ds(pl.multiple_of((rank ^ j) * rows, 16), rows)],
            sems.at[j],
        )
        for j, part in enumerate(parts)
    ]
    for c in copies:
        c.start()
    return copies


def stats_of(values):
    center = values - jnp.mean(values, -1, keepdims=True)
    spread = jnp.mean(center * center, -1, keepdims=True)
    inverse = lax.rsqrt(spread + 1e-05)
    return center * inverse, inverse


def turn(u, cosine, sin_a, sin_b, back=False):
    turned = pltpu.roll(u, LANES - 32, 1) * sin_a + pltpu.roll(u, 32, 1) * sin_b
    return u * cosine - turned if back else u * cosine + turned


def two_heads(pair, low_lanes):
    zero = jnp.zeros_like(pair)
    return jnp.concatenate(
        [jnp.where(low_lanes, pair, zero), jnp.where(low_lanes, zero, pair)], 0
    )


def one_pair(stacked, low_lanes):
    half = stacked.shape[0] // 2
    return jnp.where(low_lanes, stacked[:half], stacked[half:])


def attend_kernel(
    n_parts, info, x_ref, left_ref, right_ref, gain_ref, cos_ref, sa_ref, sb_ref, *rest
):
    parts = rest[:n_parts]
    q_ref, k_ref, v_ref, att_ref, p_ref, lse_ref, normed_ref, full, normed, sems = rest[n_parts:]
    block = x_ref.shape[1]
    width = x_ref.shape[2]
    span = block + 2 * HALF
    pairs = width // LANES

    @pl.when(pl.program_id(0) == 0)
    def _():
        for c in fetch(info[0], parts, full, sems):
            c.wait()

    x = jnp.concatenate([left_ref[0], x_ref[0], right_ref[0]], 0).astype(F32)
    normal, _ = stats_of(x)
    normed[...] = (normal * gain_ref[...]).astype(BF)
    normed_ref[0] = normed[HALF : HALF + block]
    low_span = lax.broadcasted_iota(jnp.int32, (QB, LANES), 1) < HEAD
    for group in range(3 * pairs // 2):
        wide = nt(normed[...], full[group * 256 : (group + 1) * 256])
        for h in range(2):
            piece = wide[:, h * LANES : (h + 1) * LANES]
            which, pair = divmod(group * 2 + h, pairs)
            cols = slice(pair * LANES, (pair + 1) * LANES)
            if which < 2:
                piece = turn(piece, cos_ref[...], sa_ref[...], sb_ref[...])
            if which == 0:
                q_ref[0, :, cols] = (piece.astype(BF).astype(F32) * HEAD**-0.5).astype(BF)
            elif which == 1:
                k_ref[0, :, cols] = piece.astype(BF)
            else:
                v_ref[0, :, cols] = piece.astype(BF)
    query = lax.broadcasted_iota(jnp.int32, (QB, QB + 2 * HALF), 0)
    key = lax.broadcasted_iota(jnp.int32, (QB, QB + 2 * HALF), 1)
    lane = lax.broadcasted_iota(jnp.int32, (QB, LANES), 1)
    for qb in range(block // QB):
        place = info[1] * block + qb * QB - HALF + key
        allowed = (key >= query) & (key <= query + 2 * HALF) & (place >= 0) & (place < info[2])
        bias = jnp.where(allowed, 0.0, -1e30).astype(F32)
        bias = jnp.concatenate([bias, bias], 0)
        totals = jnp.zeros((QB, LANES), F32)
        own = slice(HALF + qb * QB, HALF + (qb + 1) * QB)
        keys = slice(qb * QB, (qb + 1) * QB + 2 * HALF)
        for pair in range(pairs):
            cols = slice(pair * LANES, (pair + 1) * LANES)
            scores = nt(two_heads(q_ref[0, own, cols], low_span), k_ref[0, keys, cols]) + bias
            top = jnp.max(scores, -1, keepdims=True)
            exps = jnp.exp(scores - top)
            total = jnp.sum(exps, -1, keepdims=True)
            soft = (exps * (1.0 / total)).astype(BF)
            p_ref[0, pair, qb] = soft
            att = one_pair(nn(soft, v_ref[0, keys, cols]), low_span)
            att_ref[0, qb * QB : (qb + 1) * QB, cols] = att.astype(BF)
            lse = top + jnp.log(total)
            totals = jnp.where(lane == 2 * pair, lse[:QB], totals)
            totals = jnp.where(lane == 2 * pair + 1, lse[QB:], totals)
        lse_ref[0, qb * QB : (qb + 1) * QB] = totals


def attend(info, x, left, right, gain, tables, parts):
    seqs, block, width = x.shape
    span = block + 2 * HALF
    pairs = width // LANES
    n = len(parts)
    rows = parts[0].shape[0]

    def seq(shape):
        return pl.BlockSpec((1,) + shape, lambda s, _: (s,) + (0,) * len(shape))

    def whole(shape):
        return pl.BlockSpec(shape, lambda s, _: (0,) * len(shape))

    table = whole((span, LANES))
    out = lambda *shape, t=BF: jax.ShapeDtypeStruct((seqs,) + shape, t)
    score_shape = (pairs, block // QB, 2 * QB, QB + 2 * HALF)
    return pl.pallas_call(
        functools.partial(attend_kernel, n),
        grid_spec=pltpu.PrefetchScalarGridSpec(
            num_scalar_prefetch=1,
            grid=(seqs,),
            in_specs=[
                seq((block, width)),
                seq((HALF, width)),
                seq((HALF, width)),
                whole((1, width)),
                table,
                table,
                table,
            ]
            + [ANY] * n,
            out_specs=[
                seq((span, width)),
                seq((span, width)),
                seq((span, width)),
                seq((block, width)),
                seq(score_shape),
                seq((block, LANES)),
                seq((block, width)),
            ],
            scratch_shapes=[
                pltpu.VMEM((n * rows, width), BF),
                pltpu.VMEM((span, width), BF),
                pltpu.SemaphoreType.DMA((n,)),
            ],
        ),
        out_shape=[
            out(span, width),
            out(span, width),
            out(span, width),
            out(block, width),
            out(*score_shape),
            out(block, LANES, t=F32),
            out(block, width),
        ],
        compiler_params=params(),
        cost_estimate=cost(seqs * span * width * width * 8, 30e6, 4e6),
        name="attend",
    )(info, x, left, right, gain, *tables, *parts)


def feed_kernel(
    n, hidden, info, x_ref, att_ref, cot_ref, lse_ref, gain_ref, ind_ref, *rest
):
    out_parts, in_parts, down_parts = rest[:n], rest[n : 2 * n], rest[2 * n : 3 * n]
    (
        output_ref,
        normed_ref,
        mixed_ref,
        inner_ref,
        grad_ref,
        branch_ref,
        dom_ref,
        gain_grad_ref,
        out_w,
        in_w,
        down_w,
        sems,
    ) = rest[3 * n :]
    width = x_ref.shape[2]
    first_step = pl.program_id(0) == 0

    @pl.when(first_step)
    def _():
        copies = fetch(info[0], out_parts, out_w, sems.at[0])
        copies += fetch(info[0], in_parts, in_w, sems.at[1])
        copies += fetch(info[0], down_parts, down_w, sems.at[2])
        for c in copies:
            c.wait()
        gain_grad_ref[...] = jnp.zeros_like(gain_grad_ref)

    attended = att_ref[0]
    hidden1 = x_ref[0].astype(F32) + nn(attended, out_w[...])
    normal, inverse = stats_of(hidden1)
    normed = (normal * gain_ref[...]).astype(BF)
    normed_ref[0] = normed
    cot = cot_ref[0]
    result = hidden1
    normed_grad = jnp.zeros_like(hidden1)
    step = 384
    for c in range(hidden // step):
        one = slice(c * step, (c + 1) * step)
        two = slice(hidden + c * step, hidden + (c + 1) * step)
        first = nt(normed, in_w[one])
        second = nt(normed, in_w[two])
        phi = 0.5 * (1.0 + lax.erf(first * (1.0 / math.sqrt(2.0))))
        active = first * phi
        slope = phi + first * jnp.exp(-0.5 * first * first) * (1.0 / math.sqrt(2.0 * math.pi))
        mixed = (active * second).astype(BF)
        mixed_ref[0, :, one] = mixed
        result = result + nn(mixed, down_w[one])
        mixed_grad = nt(cot, down_w[one])
        grad_one = (mixed_grad * second * slope).astype(BF)
        grad_two = (mixed_grad * active).astype(BF)
        inner_ref[0, :, one] = grad_one
        inner_ref[0, :, two] = grad_two
        normed_grad = normed_grad + nn(grad_one, in_w[one]) + nn(grad_two, in_w[two])
    output_ref[0] = result.astype(BF)
    gain_grad_ref[...] += jnp.sum(normed_grad * normal, 0, keepdims=True)
    scaled = normed_grad * gain_ref[...]
    hidden1_grad = cot.astype(F32) + inverse * (
        scaled
        - jnp.mean(scaled, -1, keepdims=True)
        - normal * jnp.mean(scaled * normal, -1, keepdims=True)
    )
    grad_ref[0] = hidden1_grad
    branch = hidden1_grad.astype(BF)
    branch_ref[0] = branch
    att_grad = nt(branch, out_w[...]).astype(BF)
    dom_ref[0, :, :width] = att_grad
    product = att_grad.astype(F32) * attended.astype(F32)
    high = product.astype(BF)
    rest_of = (product - high.astype(F32)).astype(BF)
    delta = nn(high, ind_ref[...]) + nn(rest_of, ind_ref[...])
    both = delta + lse_ref[0]
    high = both.astype(BF)
    rest_of = both - high.astype(F32)
    dom_ref[0, :, width:] = (high.astype(F32) + pltpu.roll(rest_of, 32, 1)).astype(BF)


def feed(info, x, att, cot, lse, gain, ind, out_parts, in_parts, down_parts):
    seqs, block, width = x.shape
    n = len(out_parts)
    hidden = n * down_parts[0].shape[0]

    def seq(*shape):
        return pl.BlockSpec((1,) + shape, lambda s, _: (s,) + (0,) * len(shape))

    def whole(*shape):
        return pl.BlockSpec(shape, lambda s, _: (0,) * len(shape))

    out = lambda *shape, t=BF: jax.ShapeDtypeStruct((seqs,) + shape, t)
    return pl.pallas_call(
        functools.partial(feed_kernel, n, hidden),
        grid_spec=pltpu.PrefetchScalarGridSpec(
            num_scalar_prefetch=1,
            grid=(seqs,),
            in_specs=[
                seq(block, width),
                seq(block, width),
                seq(block, width),
                seq(block, LANES),
                whole(1, width),
                whole(width, LANES),
            ]
            + [ANY] * (3 * n),
            out_specs=[
                seq(block, width),
                seq(block, width),
                seq(block, hidden),
                seq(block, 2 * hidden),
                seq(block, width),
                seq(block, width),
                seq(block, width + LANES),
                whole(1, width),
            ],
            scratch_shapes=[
                pltpu.VMEM((width, width), BF),
                pltpu.VMEM((2 * hidden, width), BF),
                pltpu.VMEM((hidden, width), BF),
                pltpu.SemaphoreType.DMA((3, n)),
            ],
        ),
        out_shape=[
            out(block, width),
            out(block, width),
            out(block, hidden),
            out(block, 2 * hidden),
            out(block, width, t=F32),
            out(block, width),
            out(block, width + LANES),
            jax.ShapeDtypeStruct((1, width), F32),
        ],
        compiler_params=params(),
        cost_estimate=cost(seqs * block * width * (4 * width + 12 * hidden), 30e6, 3e6),
        name="feed",
    )(info, x, att, cot, lse, gain, ind, *out_parts, *in_parts, *down_parts)


def attend_back_kernel(
    q_ref,
    k_ref,
    v_ref,
    p_ref,
    dom_ref,
    left_ref,
    right_ref,
    cos_ref,
    sa_ref,
    sb_ref,
    grad_ref,
):
    block = dom_ref.shape[1]
    width = q_ref.shape[2]
    span = block + 2 * HALF
    pairs = width // LANES
    scale = HEAD**-0.5
    low = lax.broadcasted_iota(jnp.int32, (QB, LANES), 1) < HEAD
    row = lax.broadcasted_iota(jnp.int32, (QB, QB), 0)
    col = lax.broadcasted_iota(jnp.int32, (QB, QB), 1)
    seen = ((row < HALF) & (col <= row)) | ((row >= HALF) & (col >= row))
    seen = jnp.concatenate([seen, seen], 0)
    stats = jnp.concatenate([left_ref[0, :, width:], right_ref[0, :, width:]], 0).astype(F32)
    stats = stats + pltpu.roll(stats, LANES - 32, 1)
    far = slice(HALF + block, span)
    near_left = slice(HALF, 2 * HALF)
    near_right = slice(block, block + HALF)
    blocks = block // QB
    for pair in range(pairs):
        cols = slice(pair * LANES, (pair + 1) * LANES)
        key_parts, value_parts = [], []
        for qb in range(blocks):
            own = slice(HALF + qb * QB, HALF + (qb + 1) * QB)
            keys = slice(qb * QB, (qb + 1) * QB + 2 * HALF)
            rows = slice(qb * QB, (qb + 1) * QB)
            soft = p_ref[0, pair, qb]
            att_grad = two_heads(dom_ref[0, rows, cols], low)
            soft_grad = nt(att_grad, v_ref[0, keys, cols])
            soft_wide = soft.astype(F32)
            delta = jnp.sum(soft_wide * soft_grad, -1, keepdims=True)
            score_grad = (soft_wide * (soft_grad - delta)).astype(BF)
            query_grad = one_pair(nn(score_grad, k_ref[0, keys, cols]), low) * scale
            grad_ref[0, rows, cols] = turn(
                query_grad, cos_ref[rows], sa_ref[rows], sb_ref[rows], True
            ).astype(BF)
            key_parts.append(tn(score_grad, two_heads(q_ref[0, own, cols], low)))
            value_parts.append(tn(soft, att_grad))
        far_q = two_heads(jnp.concatenate([q_ref[0, :HALF, cols], q_ref[0, far, cols]], 0), low)
        far_grad = two_heads(
            jnp.concatenate([left_ref[0, :, cols], right_ref[0, :, cols]], 0), low
        )
        near_k = jnp.concatenate([k_ref[0, near_left, cols], k_ref[0, near_right, cols]], 0)
        near_v = jnp.concatenate([v_ref[0, near_left, cols], v_ref[0, near_right, cols]], 0)
        h = 2 * pair
        lse = jnp.concatenate([stats[:, h : h + 1], stats[:, h + 1 : h + 2]], 0)
        delta = jnp.concatenate([stats[:, 64 + h : 65 + h], stats[:, 65 + h : 66 + h]], 0)
        soft = jnp.where(seen, jnp.exp(jnp.where(seen, nt(far_q, near_k) - lse, 0.0)), 0.0)
        score_grad = (soft * (nt(far_grad, near_v) - delta)).astype(BF)
        far_key = tn(score_grad, far_q)
        far_value = tn(soft.astype(BF), far_grad)
        for base, pieces, extra in ((width, key_parts, far_key), (2 * width, value_parts, far_value)):
            total = jnp.zeros((span, LANES), F32)
            for qb in range(blocks):
                before, after = qb * QB, span - (qb + 1) * QB - 2 * HALF
                piece = pieces[qb]
                if before:
                    piece = jnp.concatenate([jnp.zeros((before, LANES), F32), piece], 0)
                if after:
                    piece = jnp.concatenate([piece, jnp.zeros((after, LANES), F32)], 0)
                total = total + piece
            own = total[HALF : HALF + block]
            own = jnp.concatenate(
                [
                    own[:HALF] + extra[:HALF],
                    own[HALF : block - HALF],
                    own[block - HALF :] + extra[HALF:],
                ],
                0,
            )
            if base == width:
                own = turn(own, cos_ref[...], sa_ref[...], sb_ref[...], True)
            grad_ref[0, :, base + pair * LANES : base + (pair + 1) * LANES] = own.astype(BF)


def attend_back(q, k, v, p, dom, left, right, tables):
    seqs, block, _ = dom.shape
    span, width = q.shape[1:]

    def seq(*shape):
        return pl.BlockSpec((1,) + shape, lambda s: (s,) + (0,) * len(shape))

    table = pl.BlockSpec((block, LANES), lambda s: (0, 0))
    return pl.pallas_call(
        attend_back_kernel,
        grid=(seqs,),
        in_specs=[
            seq(span, width),
            seq(span, width),
            seq(span, width),
            seq(*p.shape[1:]),
            seq(block, width + LANES),
            seq(HALF, width + LANES),
            seq(HALF, width + LANES),
            table,
            table,
            table,
        ],
        out_specs=seq(block, 3 * width),
        out_shape=jax.ShapeDtypeStruct((seqs, block, 3 * width), BF),
        compiler_params=params(),
        cost_estimate=cost(seqs * block * span * width * 12, 25e6, 1e6),
        name="attend_back",
    )(q, k, v, p, dom, left, right, *tables)


def weight_grad_kernel(n, info, lhs_ref, rhs_ref, *rest):
    parts, full, sems = rest[:n], rest[n], rest[n + 1]
    rows = parts[0].shape[0]
    step = lhs_ref.shape[1]
    i = pl.program_id(0)
    full[pl.ds(pl.multiple_of(i * step, step), step)] = tn(lhs_ref[...], rhs_ref[...]).astype(BF)

    @pl.when(i == pl.num_programs(0) - 1)
    def _():
        copies = [
            pltpu.make_async_copy(
                full.at[pl.ds(pl.multiple_of((info[0] ^ j) * rows, 16), rows)],
                part,
                sems.at[j],
            )
            for j, part in enumerate(parts)
        ]
        for c in copies:
            c.start()
        for c in copies:
            c.wait()


def weight_grad(info, lhs, rhs, n):
    tokens, m = lhs.shape
    width = rhs.shape[1]
    step = 384
    return pl.pallas_call(
        functools.partial(weight_grad_kernel, n),
        grid_spec=pltpu.PrefetchScalarGridSpec(
            num_scalar_prefetch=1,
            grid=(m // step,),
            in_specs=[
                pl.BlockSpec((tokens, step), lambda i, _: (0, i)),
                pl.BlockSpec((tokens, width), lambda i, _: (0, 0)),
            ],
            out_specs=[ANY] * n,
            scratch_shapes=[pltpu.VMEM((m, width), BF), pltpu.SemaphoreType.DMA((n,))],
        ),
        out_shape=[jax.ShapeDtypeStruct((m // n, width), BF)] * n,
        compiler_params=params(),
        cost_estimate=cost(2 * tokens * m * width, 2 * (tokens * (m + width) + m * width)),
        name="weight_grad",
    )(info, lhs, rhs)


def input_kernel(n, info, grad_ref, x_ref, gain_ref, hidden_ref, *rest):
    parts = rest[:n]
    out_ref, gain_grad_ref, full, sems = rest[n:]

    @pl.when(pl.program_id(0) == 0)
    def _():
        for c in fetch(info[0], parts, full, sems):
            c.wait()
        gain_grad_ref[...] = jnp.zeros_like(gain_grad_ref)

    normed_grad = nn(grad_ref[0], full[...])
    normal, inverse = stats_of(x_ref[0].astype(F32))
    gain_grad_ref[...] += jnp.sum(normed_grad * normal, 0, keepdims=True)
    scaled = normed_grad * gain_ref[...]
    out_ref[0] = hidden_ref[0] + inverse * (
        scaled
        - jnp.mean(scaled, -1, keepdims=True)
        - normal * jnp.mean(scaled * normal, -1, keepdims=True)
    )


def input_back(info, grad, x, gain, hidden_grad, parts):
    seqs, block, width = x.shape
    n = len(parts)

    def seq(*shape):
        return pl.BlockSpec((1,) + shape, lambda s, _: (s,) + (0,) * len(shape))

    def whole(*shape):
        return pl.BlockSpec(shape, lambda s, _: (0,) * len(shape))

    return pl.pallas_call(
        functools.partial(input_kernel, n),
        grid_spec=pltpu.PrefetchScalarGridSpec(
            num_scalar_prefetch=1,
            grid=(seqs,),
            in_specs=[
                seq(block, 3 * width),
                seq(block, width),
                whole(1, width),
                seq(block, width),
            ]
            + [ANY] * n,
            out_specs=[seq(block, width), whole(1, width)],
            scratch_shapes=[
                pltpu.VMEM((3 * width, width), BF),
                pltpu.SemaphoreType.DMA((n,)),
            ],
        ),
        out_shape=[
            jax.ShapeDtypeStruct((seqs, block, width), F32),
            jax.ShapeDtypeStruct((1, width), F32),
        ],
        compiler_params=params(),
        cost_estimate=cost(seqs * block * width * width * 6, 16e6),
        name="input_back",
    )(info, grad, x, gain, hidden_grad, *parts)


def swap(value, axis, bit):
    count = lax.axis_size(axis)
    return lax.ppermute(value, axis, [(i, i ^ bit) for i in range(count)])


def bits_of(axis):
    count = lax.axis_size(axis)
    return [1 << b for b in range(count.bit_length() - 1)]


def gather_parts(shard):
    parts = {0: shard}
    for bit in reversed(bits_of("wa")):
        for j in list(parts):
            parts[j | bit] = swap(parts[j], "wa", bit)
    return [parts[j] for j in sorted(parts)]


def plus(a, b):
    return (a.astype(F32) + b.astype(F32)).astype(BF)


def reduce_parts(parts):
    parts = dict(enumerate(parts))
    for bit in bits_of("wa"):
        for j in [j for j in parts if j & bit]:
            parts[j ^ bit] = plus(parts[j ^ bit], swap(parts.pop(j), "wa", bit))
    value = parts[0]
    rank = lax.axis_index("ctx")
    bits = bits_of("ctx")
    cuts = bits[: min(2, len(bits) - 1)]
    for bit in cuts:
        half = value.shape[0] // 2
        mine = (rank & bit) // bit
        sent = lax.dynamic_slice_in_dim(value, (1 - mine) * half, half, 0)
        kept = lax.dynamic_slice_in_dim(value, mine * half, half, 0)
        value = plus(kept, swap(sent, "ctx", bit))
    for bit in bits[len(cuts) :]:
        value = plus(value, swap(value, "ctx", bit))
    for bit in reversed(cuts):
        mine = (rank & bit) // bit
        other = swap(value, "ctx", bit)
        value = jnp.where(
            mine == 0, jnp.concatenate([value, other], 0), jnp.concatenate([other, value], 0)
        )
    return value.astype(F32)


def sum_all(value):
    for axis in ("wa", "ctx"):
        for bit in bits_of(axis):
            value = value + swap(value, axis, bit)
    return value


def neighbours(value):
    count = lax.axis_size("ctx")
    ends = count - 1
    left = lax.ppermute(value[:, -HALF:], "ctx", [(i, i + 1) for i in range(ends)])
    right = lax.ppermute(value[:, :HALF], "ctx", [(i + 1, i) for i in range(ends)])
    return left, right


def local(
    layer_input, cotangent, attention_gain, qkv_proj, out_proj, feed_gain, in_proj, down_proj
):
    seqs, block, width = layer_input.shape
    rows = seqs * block
    heads = width // HEAD
    n = lax.axis_size("wa")
    context_rank = lax.axis_index("ctx")
    seq_len = block * lax.axis_size("ctx")
    info = jnp.stack(
        [
            lax.axis_index("wa").astype(jnp.int32),
            context_rank.astype(jnp.int32),
            jnp.int32(seq_len),
        ]
    )
    left, right = neighbours(layer_input)
    qkv_parts = gather_parts(qkv_proj.T)
    out_parts = gather_parts(out_proj)
    in_parts = gather_parts(in_proj.T)
    down_parts = gather_parts(down_proj)

    frequencies = jnp.power(10000.0, -jnp.arange(0, HEAD, 2, dtype=F32) / HEAD)
    places = context_rank * block - HALF + jnp.arange(block + 2 * HALF, dtype=jnp.int32)
    angles = places.astype(F32)[:, None] * frequencies[None, :]
    cosine, sine = jnp.cos(angles), jnp.sin(angles)
    zero = jnp.zeros_like(sine)
    tables = (
        jnp.concatenate([cosine] * 4, -1),
        jnp.concatenate([-sine, zero] * 2, -1),
        jnp.concatenate([zero, sine] * 2, -1),
    )
    own_tables = tuple(t[HALF : HALF + block] for t in tables)
    lane = jnp.arange(LANES, dtype=jnp.int32)[None, :]
    head_of = jnp.arange(width, dtype=jnp.int32)[:, None] // HEAD
    ind = (lane == head_of + 64).astype(BF)

    q, k, v, attended, soft, lse, normed1 = attend(
        info, layer_input, left, right, attention_gain[None], tables, qkv_parts
    )
    output, normed2, mixed, inner_grad, hidden_grad, branch, dom, feed_gain_grad = feed(
        info,
        layer_input,
        attended,
        cotangent,
        lse,
        feed_gain[None],
        ind,
        out_parts,
        in_parts,
        down_parts,
    )
    left_grad, right_grad = neighbours(dom)
    flat = lambda a: a.reshape(rows, a.shape[-1])
    in_grad = reduce_parts(weight_grad(info, flat(inner_grad), flat(normed2), n))
    down_grad = reduce_parts(weight_grad(info, flat(mixed), flat(cotangent), n))
    out_grad = reduce_parts(weight_grad(info, flat(attended), flat(branch), n))
    projected_grad = attend_back(q, k, v, soft, dom, left_grad, right_grad, own_tables)
    qkv_grad = reduce_parts(weight_grad(info, flat(projected_grad), flat(normed1), n))
    input_grad, attention_gain_grad = input_back(
        info, projected_grad, layer_input, attention_gain[None], hidden_grad, qkv_parts
    )
    gains = sum_all(
        jnp.concatenate([attention_gain_grad, feed_gain_grad], 0).reshape(-1, LANES)
    ).reshape(2, width)
    return (
        output,
        input_grad,
        gains[0],
        gains[1],
        qkv_grad.T,
        out_grad,
        in_grad.T,
        down_grad,
    )


def solution(mesh):
    return jax.shard_map(
        local,
        mesh=mesh,
        in_specs=(
            P("wa", "ctx", None),
            P("wa", "ctx", None),
            P(),
            P(None, "wa"),
            P("wa", None),
            P(),
            P(None, "wa"),
            P("wa", None),
        ),
        out_specs=(
            P("wa", "ctx", None),
            P("wa", "ctx", None),
            P(),
            P(),
            P(None, "wa"),
            P("wa", None),
            P(None, "wa"),
            P("wa", None),
        ),
        check_vma=False,
    )
```

time: 1280 us -> 342 us (0.27)
  blocking collectives: 807 us -> 0 us
  matrix products: 132 us -> 0 us
  Pallas kernels: 0 us -> 131 us
  local copies, waits for them, and re-layouts: 80.6 us -> 7.04 us
  other arithmetic: 71.7 us -> 12.1 us
  starting transfers between devices: 13.9 us -> 54.7 us
  between operations: 15.4 us -> 1.39 us
    psum x2 -> x0, blocking collectives: 807 us -> none  [the longest x1 768 us: local(): summed = lax.psum((qkv_weight_grad, out_grad, in_grad, down_grad), 'ctx')]
    dot_general x18 -> x0, matrix products: 132 us -> none  [the longest x1 17.7 us: local(): jnp.einsum('td,fd->tf', grad_low, down_weight, preferred_element_type=jnp...]
    pallas_call x0 -> x8, Pallas kernels: none -> 131 us  [the longest x1 32.7 us: feed(): pl.pallas_call(functools.partial(feed_kernel, n, hidden), grid_spec=pltpu...]
    ppermute x4 -> x53, waiting for transfers between devices: 32.2 us -> 135 us  [the longest x49 120 us: swap(): return lax.ppermute(value, axis, [(i, i ^ bit) for i in range(count)])]
    reduce_scatter x4 -> x0, waiting for transfers between devices: 78.9 us -> none  [the longest x1 40.5 us: local(): lax.psum_scatter(summed[2].astype(jnp.bfloat16), 'wa', scatter_dimension=...]
    ppermute x4 -> x53, starting transfers between devices: 13.6 us -> 54.7 us  [the longest x49 42.7 us: swap(): return lax.ppermute(value, axis, [(i, i ^ bit) for i in range(count)])]
    reshape x9 -> x1, local copies, waits for them, and re-layouts: 33.7 us -> 0.01 us  [local(): jnp.concatenate([attention_gain_grad, feed_gain_grad], 0).reshape(-1, LANES)]
    all_gather x4 -> x0, waiting for transfers between devices: 30.6 us -> none  [the longest x1 30.6 us: local(): lax.all_gather(qkv_proj, 'wa', axis=1, tiled=True)]
  transfers between devices with their start and end apart: 12 -> 53, of which waited for: 6 -> 21; matrix products, arithmetic and copies ran while one was open for 11% -> 5% of each run, Pallas kernels for 0% -> 27%
where the time goes in v1:
time: 342 us; the launch traced here: 341 us
  waiting for transfers between devices  135 us (39%)
  Pallas kernels  131 us (38%)
  starting transfers between devices  54.7 us (16%)
  other arithmetic  12.1 us (4%)
  local copies, waits for them, and re-layouts  7.04 us (2%)
    ppermute x49, waiting for transfers between devices, swap(): return lax.ppermute(value, axis, [(i, i ^ bit) for i in range(count)])  120 us
    ppermute x49, starting transfers between devices, swap(): return lax.ppermute(value, axis, [(i, i ^ bit) for i in range(count)])  42.7 us
    pallas_call x1, Pallas kernels, feed(): pl.pallas_call(functools.partial(feed_kernel, n, hidden), grid_spec=pltpu...  32.7 us
    pallas_call x4, Pallas kernels, weight_grad(): pl.pallas_call(functools.partial(weight_grad_kernel, n), grid_spec=pltpu....  31.7 us
    pallas_call x1, Pallas kernels, attend_back(): pl.pallas_call(attend_back_kernel, grid=(seqs,), in_specs=[seq(span, widt...  29.7 us
    pallas_call x1, Pallas kernels, attend(): pl.pallas_call(functools.partial(attend_kernel, n), grid_spec=pltpu.Prefe...  25.6 us
    pallas_call x1, Pallas kernels, input_back(): pl.pallas_call(functools.partial(input_kernel, n), grid_spec=pltpu.Prefet...  11.6 us
    ppermute x2, waiting for transfers between devices, neighbours(): lax.ppermute(value[:, -HALF:], 'ctx', [(i, i + 1) for i in range(ends)])  10.3 us
  transfers between devices with their start and end apart: 53, of which 21 were waited for; matrix products, arithmetic and copies ran while one was open for 5% of the time, Pallas kernels for 27%

profile of v1, /device:TPU:0, one launch (start us, length us, event | category | flops | bytes accessed | tf_op | source)
XLA Modules:
  0.0 341.3 jit_solution(11994148356313748855)
XLA Ops:
  8.5 15.9 %collective-permute-done.3.rest_2_ = bf16[576,768]{1,0:T(8,128)(2,1)S(1)} collective-permute-done((bf16[576,768]{1,0:T(8,128)(2,1)}, bf16[576,768]{1,0:T(8,128)(2,1)S(1)}, u32[]{:S(2)}, u32[]{:S(2)}) %collective-permute-start.3) | collective-permute-done | bytes 884768 | tf_op jit(solution)/shard_map/ppermute | solution.py:567
  25.2 5.5 %collective-permute-done.6.rest_2_ = bf16[192,768]{1,0:T(8,128)(2,1)S(1)} collective-permute-done((bf16[192,768]{1,0:T(8,128)(2,1)}, bf16[192,768]{1,0:T(8,128)(2,1)S(1)}, u32[]{:S(2)}, u32[]{:S(2)}) %collective-permute-start.6) | collective-permute-done | bytes 294944 | tf_op jit(solution)/shard_map/ppermute | solution.py:567
  30.7 4.7 %collective-permute-start = (bf16[4,64,768]{2,1,0:T(8,128)(2,1)S(1)}, bf16[4,64,768]{2,1,0:T(8,128)(2,1)}, u32[]{:S(2)}, u32[]{:S(2)}) collective-permute-start(bf16[4,64,768]{2,1,0:T(8,128)(2,1)S(1)} %get-tuple-element.77), channel_id=1, source_target_pairs={{0,4},{4,8},{8,12},{12,16},{16,20},{20,24},{24,28},{1,5},{5,9},{9,... | collective-permute-start | bytes 1179656 | tf_op jit(solution)/shard_map/ppermute | solution.py:623
  41.0 8.7 %collective-permute-done.9.rest_6_ = bf16[576,768]{1,0:T(8,128)(2,1)} collective-permute-done((bf16[576,768]{1,0:T(8,128)(2,1)}, bf16[576,768]{1,0:T(8,128)(2,1)}, u32[]{:S(2)}, u32[]{:S(2)}) %collective-permute-start.9) | collective-permute-done | bytes 884768 | tf_op jit(solution)/shard_map/ppermute | solution.py:567
  50.6 7.7 %collective-permute-done.12.rest_10_ = bf16[288,768]{1,0:T(8,128)(2,1)S(1)} collective-permute-done((bf16[288,768]{1,0:T(8,128)(2,1)}, bf16[288,768]{1,0:T(8,128)(2,1)S(1)}, u32[]{:S(2)}, u32[]{:S(2)}) %collective-permute-start.12) | collective-permute-done | bytes 442400 | tf_op jit(solution)/shard_map/ppermute | solution.py:567
  58.9 25.6 %attend.1 = (bf16[4,384,768]{2,1,0:T(8,128)(2,1)}, bf16[4,384,768]{2,1,0:T(8,128)(2,1)}, bf16[4,384,768]{2,1,0:T(8,128)(2,1)}, bf16[4,256,768]{2,1,0:T(8,128)(2,...) custom-call(s32[3]{0:T(128)} %pad_add_fusion.info, ...), custom_call_target="tpu_custom_call" | custom-call | flops 7247757312 | bytes 30000000 | tf_op jit(solution)/shard_map/attend/pallas_call | solution.py:161
  85.6 32.7 %feed.1 = (bf16[4,256,768]{2,1,0:T(8,128)(2,1)}, bf16[4,256,768]{2,1,0:T(8,128)(2,1)}, bf16[4,256,1152]{2,1,0:T(8,128)(2,1)}, bf16[4,256,2304]{2,1,0:T(8,128)(2,...) custom-call(s32[3]{0:T(128)} %pad_add_fusion.info, ...), custom_call_target="tpu_custom_call" | custom-call | flops 13287555072 | bytes 30000000 | tf_op jit(solution)/shard_map/feed/pallas_call | solution.py:297
  118.4 5.2 %weight_grad.5 = (bf16[192,768]{1,0:T(8,128)(2,1)}, bf16[192,768]{1,0:T(8,128)(2,1)}, bf16[192,768]{1,0:T(8,128)(2,1)}, bf16[192,768]{1,0:T(8,128)(2,1)}) custom-call(s32[3]{0:T(128)} %pad_add_fusion.info, bf16[1024,768]{1,0:T(8,128)(2,1)} %bitcast.33, bf16[1024,768]{1,0:T(8,128)(2,1)} %bitcast.34), custom_call_target="tpu_custom_call" | custom-call | flops 1207959552 | bytes 4325376 | tf_op jit(solution)/shard_map/weight_grad/pallas_call | solution.py:487
  125.5 4.8 %collective-permute-start.14 = (bf16[4,64,896]{2,1,0:T(8,128)(2,1)S(1)}, bf16[4,64,896]{2,1,0:T(8,128)(2,1)S(1)}, u32[]{:S(2)}, u32[]{:S(2)}) collective-permute-start(bf16[4,64,896]{2,1,0:T(8,128)(2,1)S(1)} %get-tuple-element.75), channel_id=1, source_target_pairs={{0,4},{4,8},{8,12},{12,16},{16,20},{20,24},{24,28},{1,5},{5,9},{9,... | collective-permute-start | bytes 1376264 | tf_op jit(solution)/shard_map/ppermute | solution.py:623
  134.1 4.6 %collective-permute-done.15.right_ref = bf16[4,64,896]{2,1,0:T(8,128)(2,1)S(1)} collective-permute-done((bf16[4,64,896]{2,1,0:T(8,128)(2,1)S(1)}, bf16[4,64,896]{2,1,0:T(8,128)(2,1)S(1)}, u32[]{:S(2)}, u32[]{:S(2)}) %collective-permute-start.15) | collective-permute-done | bytes 458784 | tf_op jit(solution)/shard_map/ppermute | solution.py:624
  138.8 10.0 %collective-permute-done.14.left_ref = bf16[4,64,896]{2,1,0:T(8,128)(2,1)S(1)} collective-permute-done((bf16[4,64,896]{2,1,0:T(8,128)(2,1)S(1)}, bf16[4,64,896]{2,1,0:T(8,128)(2,1)S(1)}, u32[]{:S(2)}, u32[]{:S(2)}) %collective-permute-start.14) | collective-permute-done | bytes 458784 | tf_op jit(solution)/shard_map/ppermute | solution.py:623
  149.5 29.7 %attend_back.1.grad_ref = bf16[4,256,2304]{2,1,0:T(8,128)(2,1)} custom-call(bf16[4,384,768]{2,1,0:T(8,128)(2,1)} %get-tuple-element.44.q_ref, bf16[4,384,768]{2,1,0:T(8,128)(2,1)} %get-tuple-element.45.k_ref, bf16[4,384,768]{2,1,0:T(8,128)(2,1)} %get-tuple-element.46.v_ref, bf16[4,6,2,256,256]{4,3,2,1,0:T(8,128)(2,1)} %get-tuple-element.47.p_ref, ...), custom_call_target="tpu_custom_call" | custom-call | flops 3623878656 | bytes 25000000 | tf_op jit(solution)/shard_map/attend_back/pallas_call | solution.py:437
  179.3 11.6 %input_back.1 = (f32[4,256,768]{2,1,0:T(8,128)}, f32[1,768]{1,0:T(1,128)}) custom-call(s32[3]{0:T(128)} %pad_add_fusion.info, bf16[4,256,2304]{2,1,0:T(8,128)(2,1)} %attend_back.1.grad_ref, bf16[4,256,768]{2,1,0:T(8,128)(2,1)} %x_ref.5, f32[1,768]{1,0:T(1,128)} %broadcast_in_dim.6.gain_ref, f32[4,256,768]{2,1,0:T(8,128)} %get-tuple-element.49.hidden_ref, ...), custom_call_target="tpu_custom_call" | custom-call | flops 3623878656 | bytes 16000000 | tf_op jit(solution)/shard_map/input_back/pallas_call | solution.py:537
  194.3 6.5 %weight_grad.7 = (bf16[288,768]{1,0:T(8,128)(2,1)}, bf16[288,768]{1,0:T(8,128)(2,1)}, bf16[288,768]{1,0:T(8,128)(2,1)}, bf16[288,768]{1,0:T(8,128)(2,1)}) custom-call(s32[3]{0:T(128)} %pad_add_fusion.info, bf16[1024,1152]{1,0:T(8,128)(2,1)} %bitcast.30, bf16[1024,768]{1,0:T(8,128)(2,1)} %bitcast.21), custom_call_target="tpu_custom_call" | custom-call | flops 1811939328 | bytes 5701632 | tf_op jit(solution)/shard_map/weight_grad/pallas_call | solution.py:487
  204.1 10.0 %weight_grad.6 = (bf16[576,768]{1,0:T(8,128)(2,1)}, bf16[576,768]{1,0:T(8,128)(2,1)}, bf16[576,768]{1,0:T(8,128)(2,1)}, bf16[576,768]{1,0:T(8,128)(2,1)}) custom-call(s32[3]{0:T(128)} %pad_add_fusion.info, bf16[1024,2304]{1,0:T(8,128)(2,1)} %bitcast.29, bf16[1024,768]{1,0:T(8,128)(2,1)} %bitcast.32), custom_call_target="tpu_custom_call" | custom-call | flops 3623878656 | bytes 9830400 | tf_op jit(solution)/shard_map/weight_grad/pallas_call | solution.py:487
  222.9 10.0 %weight_grad.4 = (bf16[576,768]{1,0:T(8,128)(2,1)}, bf16[576,768]{1,0:T(8,128)(2,1)}, bf16[576,768]{1,0:T(8,128)(2,1)}, bf16[576,768]{1,0:T(8,128)(2,1)}) custom-call(s32[3]{0:T(128)} %pad_add_fusion.info, bf16[1024,2304]{1,0:T(8,128)(2,1)} %bitcast.20, bf16[1024,768]{1,0:T(8,128)(2,1)} %bitcast.31), custom_call_target="tpu_custom_call" | custom-call | flops 3623878656 | bytes 9830400 | tf_op jit(solution)/shard_map/weight_grad/pallas_call | solution.py:487
  236.9 5.5 %collective-permute-done.48 = bf16[144,768]{1,0:T(8,128)(2,1)S(1)} collective-permute-done((bf16[144,768]{1,0:T(8,128)(2,1)S(1)}, bf16[144,768]{1,0:T(8,128)(2,1)S(1)}, u32[]{:S(2)}, u32[]{:S(2)}) %collective-permute-start.48) | collective-permute-done | bytes 221216 | tf_op jit(solution)/shard_map/ppermute | solution.py:567
  251.9 13.0 %collective-permute-done.39 = bf16[576,768]{1,0:T(8,128)(2,1)S(1)} collective-permute-done((bf16[576,768]{1,0:T(8,128)(2,1)S(1)}, bf16[576,768]{1,0:T(8,128)(2,1)S(1)}, u32[]{:S(2)}, u32[]{:S(2)}) %collective-permute-start.39) | collective-permute-done | bytes 884768 | tf_op jit(solution)/shard_map/ppermute | solution.py:567
  267.1 15.3 %collective-permute-done.23 = bf16[576,768]{1,0:T(8,128)(2,1)S(1)} collective-permute-done((bf16[576,768]{1,0:T(8,128)(2,1)S(1)}, bf16[576,768]{1,0:T(8,128)(2,1)S(1)}, u32[]{:S(2)}, u32[]{:S(2)}) %collective-permute-start.23) | collective-permute-done | bytes 884768 | tf_op jit(solution)/shard_map/ppermute | solution.py:567
  286.7 6.8 %collective-permute-done.24 = bf16[288,768]{1,0:T(8,128)(2,1)S(1)} collective-permute-done((bf16[288,768]{1,0:T(8,128)(2,1)S(1)}, bf16[288,768]{1,0:T(8,128)(2,1)S(1)}, u32[]{:S(2)}, u32[]{:S(2)}) %collective-permute-start.24) | collective-permute-done | bytes 442400 | tf_op jit(solution)/shard_map/ppermute | solution.py:567
  296.2 6.3 %collective-permute-done.25 = bf16[144,768]{1,0:T(8,128)(2,1)S(1)} collective-permute-done((bf16[144,768]{1,0:T(8,128)(2,1)S(1)}, bf16[144,768]{1,0:T(8,128)(2,1)S(1)}, u32[]{:S(2)}, u32[]{:S(2)}) %collective-permute-start.25) | collective-permute-done | bytes 221216 | tf_op jit(solution)/shard_map/ppermute | solution.py:567
  303.2 7.0 %collective-permute-done.42 = bf16[144,768]{1,0:T(8,128)(2,1)S(1)} collective-permute-done((bf16[144,768]{1,0:T(8,128)(2,1)S(1)}, bf16[144,768]{1,0:T(8,128)(2,1)S(1)}, u32[]{:S(2)}, u32[]{:S(2)}) %collective-permute-start.42) | collective-permute-done | bytes 221216 | tf_op jit(solution)/shard_map/ppermute | solution.py:567
  325.1 7.4 %collective-permute-done.44 = bf16[288,768]{1,0:T(8,128)(2,1)S(1)} collective-permute-done((bf16[288,768]{1,0:T(8,128)(2,1)S(1)}, bf16[288,768]{1,0:T(8,128)(2,1)S(1)}, u32[]{:S(2)}, u32[]{:S(2)}) %collective-permute-start.44) | collective-permute-done | bytes 442400 | tf_op jit(solution)/shard_map/ppermute | solution.py:567
  333.9 6.1 %collective-permute-done.28 = bf16[288,768]{1,0:T(8,128)(2,1)S(1)} collective-permute-done((bf16[288,768]{1,0:T(8,128)(2,1)S(1)}, bf16[288,768]{1,0:T(8,128)(2,1)S(1)}, u32[]{:S(2)}, u32[]{:S(2)}) %collective-permute-start.28) | collective-permute-done | bytes 442400 | tf_op jit(solution)/shard_map/ppermute | solution.py:567
  (204 shorter events, 79.2 us)
Async XLA Ops:
  0.7 23.7 %collective-permute-start.3 = (bf16[576,768]{1,0:T(8,128)(2,1)}, bf16[576,768]{1,0:T(8,128)(2,1)S(1)}, u32[]{:S(2)}, u32[]{:S(2)}) collective-permute-start(bf16[576,768]{1,0:T(8,128)(2,1)} %bitcast.25), channel_id=1, source_target_pairs={{0,2},{1,3},{2,0},{3,1},{4,6},{5,7},{6,4},{7,5},{8,10},{9,11},{10,... | collective-permute-start | bytes 2654216 | tf_op jit(solution)/shard_map/ppermute | solution.py:567
  3.7 27.0 %collective-permute-start.6 = (bf16[192,768]{1,0:T(8,128)(2,1)}, bf16[192,768]{1,0:T(8,128)(2,1)S(1)}, u32[]{:S(2)}, u32[]{:S(2)}) collective-permute-start(bf16[192,768]{1,0:T(8,128)(2,1)} %rest_0_.1), channel_id=1, source_target_pairs={{0,2},{1,3},{2,0},{3,1},{4,6},{5,7},{6,4},{7,5},{8,10},{9,11},{10,... | collective-permute-start | bytes 884744 | tf_op jit(solution)/shard_map/ppermute | solution.py:567
  3.8 54.5 %collective-permute-start.2 = (bf16[576,768]{1,0:T(8,128)(2,1)}, bf16[576,768]{1,0:T(8,128)(2,1)}, u32[]{:S(2)}, u32[]{:S(2)}) collective-permute-start(bf16[576,768]{1,0:T(8,128)(2,1)} %bitcast.26), channel_id=1, source_target_pairs={{0,1},{1,0},{2,3},{3,2},{4,5},{5,4},{6,7},{7,6},{8,9},{9,8},{10,11... | collective-permute-start | bytes 2654216 | tf_op jit(solution)/shard_map/ppermute | solution.py:567
  4.2 45.6 %collective-permute-start.9 = (bf16[576,768]{1,0:T(8,128)(2,1)}, bf16[576,768]{1,0:T(8,128)(2,1)}, u32[]{:S(2)}, u32[]{:S(2)}) collective-permute-start(bf16[576,768]{1,0:T(8,128)(2,1)} %bitcast.22), channel_id=1, source_target_pairs={{0,2},{1,3},{2,0},{3,1},{4,6},{5,7},{6,4},{7,5},{8,10},{9,11},{10,... | collective-permute-start | bytes 2654216 | tf_op jit(solution)/shard_map/ppermute | solution.py:567
  7.2 30.3 %collective-permute-start.1 = (bf16[4,64,768]{2,1,0:T(8,128)(2,1)S(1)}, bf16[4,64,768]{2,1,0:T(8,128)(2,1)}, u32[]{:S(2)}, u32[]{:S(2)}) collective-permute-start(bf16[4,64,768]{2,1,0:T(8,128)(2,1)S(1)} %get-tuple-element.76), channel_id=1, source_target_pairs={{4,0},{8,4},{12,8},{16,12},{20,16},{24,20},{28,24},{5,1},{9,5},{13... | collective-permute-start | bytes 1179656 | tf_op jit(solution)/shard_map/ppermute | solution.py:624
  24.4 34.4 %collective-permute-start.4 = (bf16[576,768]{1,0:T(8,128)(2,1)S(1)}, bf16[576,768]{1,0:T(8,128)(2,1)}, u32[]{:S(2)}, u32[]{:S(2)}) collective-permute-start(bf16[576,768]{1,0:T(8,128)(2,1)S(1)} %collective-permute-done.3.rest_2_), channel_id=1, source_target_pairs={{0,1},{1,0},{2,3},{3,2},{4,5},{5,4},{6,7},{7,6},{8,9},{9,8},{10,11... | collective-permute-start | bytes 2654216 | tf_op jit(solution)/shard_map/ppermute | solution.py:567
  37.5 20.8 %collective-permute-start.12 = (bf16[288,768]{1,0:T(8,128)(2,1)}, bf16[288,768]{1,0:T(8,128)(2,1)S(1)}, u32[]{:S(2)}, u32[]{:S(2)}) collective-permute-start(bf16[288,768]{1,0:T(8,128)(2,1)} %rest_8_.1), channel_id=1, source_target_pairs={{0,2},{1,3},{2,0},{3,1},{4,6},{5,7},{6,4},{7,5},{8,10},{9,11},{10,... | collective-permute-start | bytes 1327112 | tf_op jit(solution)/shard_map/ppermute | solution.py:567
  41.0 43.6 %collective-permute-start.8 = (bf16[576,768]{1,0:T(8,128)(2,1)S(1)}, bf16[576,768]{1,0:T(8,128)(2,1)S(1)}, u32[]{:S(2)}, u32[]{:S(2)}) collective-permute-start(bf16[576,768]{1,0:T(8,128)(2,1)S(1)} %bitcast.24), channel_id=1, source_target_pairs={{0,1},{1,0},{2,3},{3,2},{4,5},{5,4},{6,7},{7,6},{8,9},{9,8},{10,11... | collective-permute-start | bytes 2654216 | tf_op jit(solution)/shard_map/ppermute | solution.py:567
  49.8 34.9 %collective-permute-start.10 = (bf16[576,768]{1,0:T(8,128)(2,1)}, bf16[576,768]{1,0:T(8,128)(2,1)}, u32[]{:S(2)}, u32[]{:S(2)}) collective-permute-start(bf16[576,768]{1,0:T(8,128)(2,1)} %collective-permute-done.9.rest_6_), channel_id=1, source_target_pairs={{0,1},{1,0},{2,3},{3,2},{4,5},{5,4},{6,7},{7,6},{8,9},{9,8},{10,11... | collective-permute-start | bytes 2654216 | tf_op jit(solution)/shard_map/ppermute | solution.py:567
  58.3 26.3 %collective-permute-start.11 = (bf16[288,768]{1,0:T(8,128)(2,1)S(1)}, bf16[288,768]{1,0:T(8,128)(2,1)}, u32[]{:S(2)}, u32[]{:S(2)}) collective-permute-start(bf16[288,768]{1,0:T(8,128)(2,1)S(1)} %copy-done.21), channel_id=1, source_target_pairs={{0,1},{1,0},{2,3},{3,2},{4,5},{5,4},{6,7},{7,6},{8,9},{9,8},{10,11... | collective-permute-start | bytes 1327112 | tf_op jit(solution)/shard_map/ppermute | solution.py:567
  58.3 26.3 %collective-permute-start.7 = (bf16[192,768]{1,0:T(8,128)(2,1)}, bf16[192,768]{1,0:T(8,128)(2,1)S(1)}, u32[]{:S(2)}, u32[]{:S(2)}) collective-permute-start(bf16[192,768]{1,0:T(8,128)(2,1)} %copy-done.25), channel_id=1, source_target_pairs={{0,1},{1,0},{2,3},{3,2},{4,5},{5,4},{6,7},{7,6},{8,9},{9,8},{10,11... | collective-permute-start | bytes 884744 | tf_op jit(solution)/shard_map/ppermute | solution.py:567
  58.8 25.8 %collective-permute-start.13 = (bf16[288,768]{1,0:T(8,128)(2,1)S(1)}, bf16[288,768]{1,0:T(8,128)(2,1)}, u32[]{:S(2)}, u32[]{:S(2)}) collective-permute-start(bf16[288,768]{1,0:T(8,128)(2,1)S(1)} %collective-permute-done.12.rest_10_), channel_id=1, source_target_pairs={{0,1},{1,0},{2,3},{3,2},{4,5},{5,4},{6,7},{7,6},{8,9},{9,8},{10,11... | collective-permute-start | bytes 1327112 | tf_op jit(solution)/shard_map/ppermute | solution.py:567
  125.5 23.2 %collective-permute-start.14 = (bf16[4,64,896]{2,1,0:T(8,128)(2,1)S(1)}, bf16[4,64,896]{2,1,0:T(8,128)(2,1)S(1)}, u32[]{:S(2)}, u32[]{:S(2)}) collective-permute-start(bf16[4,64,896]{2,1,0:T(8,128)(2,1)S(1)} %get-tuple-element.75), channel_id=1, source_target_pairs={{0,4},{4,8},{8,12},{12,16},{16,20},{20,24},{24,28},{1,5},{5,9},{9,... | collective-permute-start | bytes 1376264 | tf_op jit(solution)/shard_map/ppermute | solution.py:623
  132.2 71.6 %collective-permute-start.29 = (bf16[192,768]{1,0:T(8,128)(2,1)S(1)}, bf16[192,768]{1,0:T(8,128)(2,1)S(1)}, u32[]{:S(2)}, u32[]{:S(2)}) collective-permute-start(bf16[192,768]{1,0:T(8,128)(2,1)S(1)} %copy-done.23), channel_id=1, source_target_pairs={{0,1},{1,0},{2,3},{3,2},{4,5},{5,4},{6,7},{7,6},{8,9},{9,8},{10,11... | collective-permute-start | bytes 884744 | tf_op jit(solution)/shard_map/ppermute | solution.py:567
  132.3 71.5 %collective-permute-start.31 = (bf16[192,768]{1,0:T(8,128)(2,1)S(1)}, bf16[192,768]{1,0:T(8,128)(2,1)S(1)}, u32[]{:S(2)}, u32[]{:S(2)}) collective-permute-start(bf16[192,768]{1,0:T(8,128)(2,1)S(1)} %add_convert_fusion.12), channel_id=1, source_target_pairs={{0,2},{1,3},{2,0},{3,1},{4,6},{5,7},{6,4},{7,5},{8,10},{9,11},{10,... | collective-permute-start | bytes 884744 | tf_op jit(solution)/shard_map/ppermute | solution.py:567
  200.8 32.7 %collective-permute-start.45 = (bf16[288,768]{1,0:T(8,128)(2,1)}, bf16[288,768]{1,0:T(8,128)(2,1)S(1)}, u32[]{:S(2)}, u32[]{:S(2)}) collective-permute-start(bf16[288,768]{1,0:T(8,128)(2,1)} %get-tuple-element.71), channel_id=1, source_target_pairs={{0,1},{1,0},{2,3},{3,2},{4,5},{5,4},{6,7},{7,6},{8,9},{9,8},{10,11... | collective-permute-start | bytes 1327112 | tf_op jit(solution)/shard_map/ppermute | solution.py:567
  214.1 20.5 %collective-permute-start.38 = (bf16[576,768]{1,0:T(8,128)(2,1)}, bf16[576,768]{1,0:T(8,128)(2,1)S(1)}, u32[]{:S(2)}, u32[]{:S(2)}) collective-permute-start(bf16[576,768]{1,0:T(8,128)(2,1)} %get-tuple-element.68), channel_id=1, source_target_pairs={{0,1},{1,0},{2,3},{3,2},{4,5},{5,4},{6,7},{7,6},{8,9},{9,8},{10,11... | collective-permute-start | bytes 2654216 | tf_op jit(solution)/shard_map/ppermute | solution.py:567
  233.0 34.0 %collective-permute-start.21 = (bf16[576,768]{1,0:T(8,128)(2,1)}, bf16[576,768]{1,0:T(8,128)(2,1)S(1)}, u32[]{:S(2)}, u32[]{:S(2)}) collective-permute-start(bf16[576,768]{1,0:T(8,128)(2,1)} %get-tuple-element.55), channel_id=1, source_target_pairs={{0,1},{1,0},{2,3},{3,2},{4,5},{5,4},{6,7},{7,6},{8,9},{9,8},{10,11... | collective-permute-start | bytes 2654216 | tf_op jit(solution)/shard_map/ppermute | solution.py:567
  242.3 22.5 %collective-permute-start.39 = (bf16[576,768]{1,0:T(8,128)(2,1)S(1)}, bf16[576,768]{1,0:T(8,128)(2,1)S(1)}, u32[]{:S(2)}, u32[]{:S(2)}) collective-permute-start(bf16[576,768]{1,0:T(8,128)(2,1)S(1)} %add_convert_fusion.1), channel_id=1, source_target_pairs={{0,2},{1,3},{2,0},{3,1},{4,6},{5,7},{6,4},{7,5},{8,10},{9,11},{10,... | collective-permute-start | bytes 2654216 | tf_op jit(solution)/shard_map/ppermute | solution.py:567
  243.2 39.2 %collective-permute-start.23 = (bf16[576,768]{1,0:T(8,128)(2,1)S(1)}, bf16[576,768]{1,0:T(8,128)(2,1)S(1)}, u32[]{:S(2)}, u32[]{:S(2)}) collective-permute-start(bf16[576,768]{1,0:T(8,128)(2,1)S(1)} %add_convert_fusion.4), channel_id=1, source_target_pairs={{0,2},{1,3},{2,0},{3,1},{4,6},{5,7},{6,4},{7,5},{8,10},{9,11},{10,... | collective-permute-start | bytes 2654216 | tf_op jit(solution)/shard_map/ppermute | solution.py:567
  249.6 73.7 %collective-permute-start.36 = (bf16[96,768]{1,0:T(8,128)(2,1)S(1)}, bf16[96,768]{1,0:T(8,128)(2,1)S(1)}, u32[]{:S(2)}, u32[]{:S(2)}) collective-permute-start(bf16[96,768]{1,0:T(8,128)(2,1)S(1)} %maximum_select_fusion.7), channel_id=1, source_target_pairs={{0,4},{4,0},{8,12},{12,8},{16,20},{20,16},{24,28},{28,24},{1,5},{5... | collective-permute-start | bytes 442376 | tf_op jit(solution)/shard_map/ppermute | solution.py:567
  251.4 33.0 %collective-permute-start.50 = (bf16[72,768]{1,0:T(8,128)(2,1)S(1)}, bf16[72,768]{1,0:T(8,128)(2,1)S(1)}, u32[]{:S(2)}, u32[]{:S(2)}) collective-permute-start(bf16[72,768]{1,0:T(8,128)(2,1)S(1)} %add_convert_fusion.21), channel_id=1, source_target_pairs={{0,16},{4,20},{8,24},{12,28},{16,0},{20,4},{24,8},{28,12},{1,17},{... | collective-permute-start | bytes 331784 | tf_op jit(solution)/shard_map/ppermute | solution.py:567
  265.2 19.6 %collective-permute-start.40 = (bf16[288,768]{1,0:T(8,128)(2,1)S(1)}, bf16[288,768]{1,0:T(8,128)(2,1)S(1)}, u32[]{:S(2)}, u32[]{:S(2)}) collective-permute-start(bf16[288,768]{1,0:T(8,128)(2,1)S(1)} %constant_dynamic-slice_fusion.3), channel_id=1, source_target_pairs={{0,4},{4,0},{8,12},{12,8},{16,20},{20,16},{24,28},{28,24},{1,5},{5... | collective-permute-start | bytes 1327112 | tf_op jit(solution)/shard_map/ppermute | solution.py:567
  284.4 30.2 %collective-permute-start.51 = (bf16[72,768]{1,0:T(8,128)(2,1)S(1)}, bf16[72,768]{1,0:T(8,128)(2,1)S(1)}, u32[]{:S(2)}, u32[]{:S(2)}) collective-permute-start(bf16[72,768]{1,0:T(8,128)(2,1)S(1)} %add_convert_fusion.20), channel_id=1, source_target_pairs={{0,8},{4,12},{8,0},{12,4},{16,24},{20,28},{24,16},{28,20},{1,9},{5... | collective-permute-start | bytes 331784 | tf_op jit(solution)/shard_map/ppermute | solution.py:567
  (56 other events, 687.0 us)

commit v2 on v1

--- a/solution.py
+++ b/solution.py
@@ -42,19 +42,26 @@
     )
 
 
-def fetch(rank, parts, full, sems):
-    rows = parts[0].shape[0]
-    copies = [
-        pltpu.make_async_copy(
-            part,
-            full.at[pl.ds(pl.multiple_of((rank ^ j) * rows, 16), rows)],
-            sems.at[j],
-        )
-        for j, part in enumerate(parts)
-    ]
+def start_all(copies):
     for c in copies:
         c.start()
-    return copies
+    for c in copies:
+        c.wait()
+
+
+def load(rank, parts, full, sems, sizes):
+    copies, taken, base = [], 0, 0
+    for rows in sizes:
+        for j, part in enumerate(parts):
+            row = pl.multiple_of(base + (rank ^ j) * rows, 16)
+            copies.append(
+                pltpu.make_async_copy(
+                    part.at[pl.ds(taken, rows)], full.at[pl.ds(row, rows)], sems.at[len(copies)]
+                )
+            )
+        taken += rows
+        base += rows * len(parts)
+    start_all(copies)
 
 
 def stats_of(values):
@@ -82,10 +89,10 @@
 
 
 def attend_kernel(
-    n_parts, info, x_ref, left_ref, right_ref, gain_ref, cos_ref, sa_ref, sb_ref, *rest
+    info, x_ref, left_ref, right_ref, gain_ref, cos_ref, sa_ref, sb_ref, *rest
 ):
-    parts = rest[:n_parts]
-    q_ref, k_ref, v_ref, att_ref, p_ref, lse_ref, normed_ref, full, normed, sems = rest[n_parts:]
+    parts = rest[:4]
+    q_ref, k_ref, v_ref, att_ref, p_ref, lse_ref, normed_ref, full, normed, sems = rest[4:]
     block = x_ref.shape[1]
     width = x_ref.shape[2]
     span = block + 2 * HALF
@@ -93,8 +100,7 @@
 
     @pl.when(pl.program_id(0) == 0)
     def _():
-        for c in fetch(info[0], parts, full, sems):
-            c.wait()
+        load(info[0], parts, full, sems, (parts[0].shape[0],))
 
     x = jnp.concatenate([left_ref[0], x_ref[0], right_ref[0]], 0).astype(F32)
     normal, _ = stats_of(x)
@@ -146,8 +152,6 @@
     seqs, block, width = x.shape
     span = block + 2 * HALF
     pairs = width // LANES
-    n = len(parts)
-    rows = parts[0].shape[0]
 
     def seq(shape):
         return pl.BlockSpec((1,) + shape, lambda s, _: (s,) + (0,) * len(shape))
@@ -159,7 +163,7 @@
     out = lambda *shape, t=BF: jax.ShapeDtypeStruct((seqs,) + shape, t)
     score_shape = (pairs, block // QB, 2 * QB, QB + 2 * HALF)
     return pl.pallas_call(
-        functools.partial(attend_kernel, n),
+        attend_kernel,
         grid_spec=pltpu.PrefetchScalarGridSpec(
             num_scalar_prefetch=1,
             grid=(seqs,),
@@ -172,7 +176,7 @@
                 table,
                 table,
             ]
-            + [ANY] * n,
+            + [ANY] * 4,
             out_specs=[
                 seq((span, width)),
                 seq((span, width)),
@@ -181,11 +185,11 @@
                 seq(score_shape),
                 seq((block, LANES)),
                 seq((block, width)),
+                whole((3 * width, width)),
             ],
             scratch_shapes=[
-                pltpu.VMEM((n * rows, width), BF),
                 pltpu.VMEM((span, width), BF),
-                pltpu.SemaphoreType.DMA((n,)),
+                pltpu.SemaphoreType.DMA((4,)),
             ],
         ),
         out_shape=[
@@ -196,6 +200,7 @@
             out(*score_shape),
             out(block, LANES, t=F32),
             out(block, width),
+            jax.ShapeDtypeStruct((3 * width, width), BF),
         ],
         compiler_params=params(),
         cost_estimate=cost(seqs * span * width * width * 8, 30e6, 4e6),
@@ -204,9 +209,8 @@
 
 
 def feed_kernel(
-    n, hidden, info, x_ref, att_ref, cot_ref, lse_ref, gain_ref, ind_ref, *rest
+    hidden, info, x_ref, att_ref, cot_ref, lse_ref, gain_ref, ind_ref, *rest
 ):
-    out_parts, in_parts, down_parts = rest[:n], rest[n : 2 * n], rest[2 * n : 3 * n]
     (
         output_ref,
         normed_ref,
@@ -216,21 +220,18 @@
         branch_ref,
         dom_ref,
         gain_grad_ref,
-        out_w,
-        in_w,
-        down_w,
+        full,
         sems,
-    ) = rest[3 * n :]
+    ) = rest[4:]
     width = x_ref.shape[2]
+    in_w = full.at[pl.ds(0, 2 * hidden)]
+    down_w = full.at[pl.ds(2 * hidden, hidden)]
+    out_w = full.at[pl.ds(3 * hidden, width)]
     first_step = pl.program_id(0) == 0
 
     @pl.when(first_step)
     def _():
-        copies = fetch(info[0], out_parts, out_w, sems.at[0])
-        copies += fetch(info[0], in_parts, in_w, sems.at[1])
-        copies += fetch(info[0], down_parts, down_w, sems.at[2])
-        for c in copies:
-            c.wait()
+        load(info[0], rest[:4], full, sems, (hidden // 2, hidden // 4, width // 4))
         gain_grad_ref[...] = jnp.zeros_like(gain_grad_ref)
 
     attended = att_ref[0]
@@ -282,10 +283,10 @@
     dom_ref[0, :, width:] = (high.astype(F32) + pltpu.roll(rest_of, 32, 1)).astype(BF)
 
 
-def feed(info, x, att, cot, lse, gain, ind, out_parts, in_parts, down_parts):
+def feed(info, x, att, cot, lse, gain, ind, parts):
     seqs, block, width = x.shape
-    n = len(out_parts)
-    hidden = n * down_parts[0].shape[0]
+    hidden = parts[0].shape[0] - width // 4
+    hidden = 4 * hidden // 3
 
     def seq(*shape):
         return pl.BlockSpec((1,) + shape, lambda s, _: (s,) + (0,) * len(shape))
@@ -295,7 +296,7 @@
 
     out = lambda *shape, t=BF: jax.ShapeDtypeStruct((seqs,) + shape, t)
     return pl.pallas_call(
-        functools.partial(feed_kernel, n, hidden),
+        functools.partial(feed_kernel, hidden),
         grid_spec=pltpu.PrefetchScalarGridSpec(
             num_scalar_prefetch=1,
             grid=(seqs,),
@@ -307,7 +308,7 @@
                 whole(1, width),
                 whole(width, LANES),
             ]
-            + [ANY] * (3 * n),
+            + [ANY] * 4,
             out_specs=[
                 seq(block, width),
                 seq(block, width),
@@ -319,10 +320,8 @@
                 whole(1, width),
             ],
             scratch_shapes=[
-                pltpu.VMEM((width, width), BF),
-                pltpu.VMEM((2 * hidden, width), BF),
-                pltpu.VMEM((hidden, width), BF),
-                pltpu.SemaphoreType.DMA((3, n)),
+                pltpu.VMEM((3 * hidden + width, width), BF),
+                pltpu.SemaphoreType.DMA((12,)),
             ],
         ),
         out_shape=[
@@ -338,7 +337,7 @@
         compiler_params=params(),
         cost_estimate=cost(seqs * block * width * (4 * width + 12 * hidden), 30e6, 3e6),
         name="feed",
-    )(info, x, att, cot, lse, gain, ind, *out_parts, *in_parts, *down_parts)
+    )(info, x, att, cot, lse, gain, ind, *parts)
 
 
 def attend_back_kernel(
@@ -352,8 +351,9 @@
     cos_ref,
     sa_ref,
     sb_ref,
-    grad_ref,
+    *rest,
 ):
+    grad_ref = rest[-1]
     block = dom_ref.shape[1]
     width = q_ref.shape[2]
     span = block + 2 * HALF
@@ -426,17 +426,17 @@
             grad_ref[0, :, base + pair * LANES : base + (pair + 1) * LANES] = own.astype(BF)
 
 
-def attend_back(q, k, v, p, dom, left, right, tables):
+def attend_back(q, k, v, p, dom, left, right, tables, start, count, before):
     seqs, block, _ = dom.shape
     span, width = q.shape[1:]
 
     def seq(*shape):
-        return pl.BlockSpec((1,) + shape, lambda s: (s,) + (0,) * len(shape))
+        return pl.BlockSpec((1,) + shape, lambda s: (s + start,) + (0,) * len(shape))
 
     table = pl.BlockSpec((block, LANES), lambda s: (0, 0))
     return pl.pallas_call(
         attend_back_kernel,
-        grid=(seqs,),
+        grid=(count,),
         in_specs=[
             seq(span, width),
             seq(span, width),
@@ -448,74 +448,119 @@
             table,
             table,
             table,
-        ],
+        ]
+        + [ANY] * len(before),
         out_specs=seq(block, 3 * width),
         out_shape=jax.ShapeDtypeStruct((seqs, block, 3 * width), BF),
+        input_output_aliases={10: 0} if before else {},
         compiler_params=params(),
-        cost_estimate=cost(seqs * block * span * width * 12, 25e6, 1e6),
+        cost_estimate=cost(count * block * span * width * 12, 7e6 * count, 3e5 * count),
         name="attend_back",
-    )(q, k, v, p, dom, left, right, *tables)
-
-
-def weight_grad_kernel(n, info, lhs_ref, rhs_ref, *rest):
-    parts, full, sems = rest[:n], rest[n], rest[n + 1]
-    rows = parts[0].shape[0]
-    step = lhs_ref.shape[1]
+    )(q, k, v, p, dom, left, right, *tables, *before)
+
+
+EXTRA = 32
+
+
+def weight_grad_kernel(steps, n, with_gains, info, *refs):
+    pairs = len(steps)
+    operands = refs[: 2 * pairs]
+    keep, send, full, sems = refs[-6:-2] if with_gains else refs[-4:]
     i = pl.program_id(0)
-    full[pl.ds(pl.multiple_of(i * step, step), step)] = tn(lhs_ref[...], rhs_ref[...]).astype(BF)
-
-    @pl.when(i == pl.num_programs(0) - 1)
+    last = i == pl.num_programs(0) - 1
+    stride = keep.shape[0] // (n // 2)
+    copies, done, taken = [], 0, 0
+
+    def target(j, row, rows):
+        return (send if j % 2 else keep).at[pl.ds((j // 2) * stride + row, rows)]
+
+    for a, count in enumerate(steps):
+        lhs, rhs = operands[2 * a : 2 * a + 2]
+        step = lhs.shape[1]
+
+        @pl.when((i >= done) & (i < done + count))
+        def _():
+            total = tn(lhs[...], rhs[...])
+            full[pl.ds(pl.multiple_of(i * step, step), step)] = total.astype(BF)
+            if with_gains:
+                weight = refs[2 * pairs]
+                gain_total = refs[-2]
+                part = jnp.sum(total * weight[...].astype(F32), 0, keepdims=True)
+                gain_total[...] = jnp.where(i == 0, part, gain_total[...] + part)
+
+        rows = count * step // n
+        for j in range(n):
+            source = pl.multiple_of(done * step + (info[0] ^ j) * rows, 16)
+            copies.append(
+                pltpu.make_async_copy(
+                    full.at[pl.ds(source, rows)], target(j, taken, rows), sems.at[len(copies)]
+                )
+            )
+        done += count
+        taken += rows
+    if with_gains:
+        for j in range(n):
+            copies.append(
+                pltpu.make_async_copy(refs[-1], target(j, taken, EXTRA), sems.at[len(copies)])
+            )
+
+    @pl.when(last)
     def _():
-        copies = [
-            pltpu.make_async_copy(
-                full.at[pl.ds(pl.multiple_of((info[0] ^ j) * rows, 16), rows)],
-                part,
-                sems.at[j],
+        if with_gains:
+            gain, feed_grad = refs[2 * pairs + 1 : 2 * pairs + 3]
+            gain_total, gain_rows = refs[-2:]
+            row = lax.broadcasted_iota(jnp.int32, gain_rows.shape, 0)
+            value = jnp.where(row == 0, gain_total[...] / gain[...], 0.0)
+            gain_rows[...] = jnp.where(row == 1, feed_grad[...], value).astype(BF)
+        start_all(copies)
+
+
+def weight_grad(info, pairs, n, gains=()):
+    tokens, width = pairs[0][1].shape
+    step = 384
+    steps = tuple(lhs.shape[1] // step for lhs, _ in pairs)
+    total = sum(steps)
+    specs, done = [], 0
+    for count in steps:
+        low, high = done, done + count - 1
+        specs.append(
+            pl.BlockSpec(
+                (tokens, step),
+                lambda i, _, low=low, high=high: (0, jnp.clip(i, low, high) - low),
             )
-            for j, part in enumerate(parts)
-        ]
-        for c in copies:
-            c.start()
-        for c in copies:
-            c.wait()
-
-
-def weight_grad(info, lhs, rhs, n):
-    tokens, m = lhs.shape
-    width = rhs.shape[1]
-    step = 384
+        )
+        specs.append(pl.BlockSpec((tokens, width), lambda i, _: (0, 0)))
+        done += count
+    m = total * step
+    scratch = [
+        pltpu.VMEM((m, width), BF),
+        pltpu.SemaphoreType.DMA((n * (len(pairs) + bool(gains)),)),
+    ]
+    if gains:
+        specs.append(pl.BlockSpec((step, width), lambda i, _: (i, 0)))
+        specs += [pl.BlockSpec((1, width), lambda i, _: (0, 0))] * 2
+        scratch += [pltpu.VMEM((1, width), F32), pltpu.VMEM((EXTRA, width), BF)]
+    rows = m // n + (EXTRA if gains else 0)
     return pl.pallas_call(
-        functools.partial(weight_grad_kernel, n),
+        functools.partial(weight_grad_kernel, steps, n, bool(gains)),
         grid_spec=pltpu.PrefetchScalarGridSpec(
             num_scalar_prefetch=1,
-            grid=(m // step,),
-            in_specs=[
-                pl.BlockSpec((tokens, step), lambda i, _: (0, i)),
-                pl.BlockSpec((tokens, width), lambda i, _: (0, 0)),
-            ],
-            out_specs=[ANY] * n,
-            scratch_shapes=[pltpu.VMEM((m, width), BF), pltpu.SemaphoreType.DMA((n,))],
+            grid=(total,),
+            in_specs=specs,
+            out_specs=[ANY] * 2,
+            scratch_shapes=scratch,
         ),
-        out_shape=[jax.ShapeDtypeStruct((m // n, width), BF)] * n,
+        out_shape=[jax.ShapeDtypeStruct((n // 2 * rows, width), BF)] * 2,
         compiler_params=params(),
         cost_estimate=cost(2 * tokens * m * width, 2 * (tokens * (m + width) + m * width)),
         name="weight_grad",
-    )(info, lhs, rhs)
-
-
-def input_kernel(n, info, grad_ref, x_ref, gain_ref, hidden_ref, *rest):
-    parts = rest[:n]
-    out_ref, gain_grad_ref, full, sems = rest[n:]
-
-    @pl.when(pl.program_id(0) == 0)
-    def _():
-        for c in fetch(info[0], parts, full, sems):
-            c.wait()
-        gain_grad_ref[...] = jnp.zeros_like(gain_grad_ref)
-
-    normed_grad = nn(grad_ref[0], full[...])
+    )(info, *[a for pair in pairs for a in pair], *gains)
+
+
+def input_kernel(grad_ref, x_ref, gain_ref, hidden_ref, weight_ref, *rest):
+    out_ref = rest[-1]
+    normed_grad = nn(grad_ref[0], weight_ref[...])
     normal, inverse = stats_of(x_ref[0].astype(F32))
-    gain_grad_ref[...] += jnp.sum(normed_grad * normal, 0, keepdims=True)
     scaled = normed_grad * gain_ref[...]
     out_ref[0] = hidden_ref[0] + inverse * (
         scaled
@@ -524,42 +569,33 @@
     )
 
 
-def input_back(info, grad, x, gain, hidden_grad, parts):
+def input_back(grad, x, gain, hidden_grad, weight, start, count, before):
     seqs, block, width = x.shape
-    n = len(parts)
 
     def seq(*shape):
-        return pl.BlockSpec((1,) + shape, lambda s, _: (s,) + (0,) * len(shape))
+        return pl.BlockSpec((1,) + shape, lambda s: (s + start,) + (0,) * len(shape))
 
     def whole(*shape):
-        return pl.BlockSpec(shape, lambda s, _: (0,) * len(shape))
+        return pl.BlockSpec(shape, lambda s: (0,) * len(shape))
 
     return pl.pallas_call(
-        functools.partial(input_kernel, n),
-        grid_spec=pltpu.PrefetchScalarGridSpec(
-            num_scalar_prefetch=1,
-            grid=(seqs,),
-            in_specs=[
-                seq(block, 3 * width),
-                seq(block, width),
-                whole(1, width),
-                seq(block, width),
-            ]
-            + [ANY] * n,
-            out_specs=[seq(block, width), whole(1, width)],
-            scratch_shapes=[
-                pltpu.VMEM((3 * width, width), BF),
-                pltpu.SemaphoreType.DMA((n,)),
-            ],
-        ),
-        out_shape=[
-            jax.ShapeDtypeStruct((seqs, block, width), F32),
-            jax.ShapeDtypeStruct((1, width), F32),
-        ],
+        input_kernel,
+        grid=(count,),
+        in_specs=[
+            seq(block, 3 * width),
+            seq(block, width),
+            whole(1, width),
+            seq(block, width),
+            whole(3 * width, width),
+        ]
+        + [ANY] * len(before),
+        out_specs=seq(block, width),
+        out_shape=jax.ShapeDtypeStruct((seqs, block, width), F32),
+        input_output_aliases={5: 0} if before else {},
         compiler_params=params(),
-        cost_estimate=cost(seqs * block * width * width * 6, 16e6),
+        cost_estimate=cost(count * block * width * width * 6, 4e6 * count),
         name="input_back",
-    )(info, grad, x, gain, hidden_grad, *parts)
+    )(grad, x, gain, hidden_grad, weight, *before)
 
 
 def swap(value, axis, bit):
@@ -572,49 +608,69 @@
     return [1 << b for b in range(count.bit_length() - 1)]
 
 
-def gather_parts(shard):
-    parts = {0: shard}
-    for bit in reversed(bits_of("wa")):
-        for j in list(parts):
-            parts[j | bit] = swap(parts[j], "wa", bit)
-    return [parts[j] for j in sorted(parts)]
+def tie(*values):
+    return lax.optimization_barrier(values)
 
 
 def plus(a, b):
     return (a.astype(F32) + b.astype(F32)).astype(BF)
 
 
-def reduce_parts(parts):
-    parts = dict(enumerate(parts))
-    for bit in bits_of("wa"):
-        for j in [j for j in parts if j & bit]:
-            parts[j ^ bit] = plus(parts[j ^ bit], swap(parts.pop(j), "wa", bit))
-    value = parts[0]
-    rank = lax.axis_index("ctx")
-    bits = bits_of("ctx")
-    cuts = bits[: min(2, len(bits) - 1)]
-    for bit in cuts:
-        half = value.shape[0] // 2
-        mine = (rank & bit) // bit
-        sent = lax.dynamic_slice_in_dim(value, (1 - mine) * half, half, 0)
-        kept = lax.dynamic_slice_in_dim(value, mine * half, half, 0)
-        value = plus(kept, swap(sent, "ctx", bit))
-    for bit in bits[len(cuts) :]:
-        value = plus(value, swap(value, "ctx", bit))
-    for bit in reversed(cuts):
-        mine = (rank & bit) // bit
-        other = swap(value, "ctx", bit)
-        value = jnp.where(
-            mine == 0, jnp.concatenate([value, other], 0), jnp.concatenate([other, value], 0)
-        )
-    return value.astype(F32)
-
-
-def sum_all(value):
-    for axis in ("wa", "ctx"):
-        for bit in bits_of(axis):
-            value = value + swap(value, axis, bit)
-    return value
+def swap_both(value, context_bit, bit):
+    count = lax.axis_size("wa")
+    every = lax.axis_size("ctx") * count
+    mask = context_bit * count + bit
+    return lax.ppermute(value, ("ctx", "wa"), [(i, i ^ mask) for i in range(every)])
+
+
+def reduce_steps(keep, send, far_first):
+    place = lax.axis_index("ctx") & 3
+    got = yield [swap(send, "wa", 1)]
+    both = plus(keep, got[0])
+    size = both.shape[0] // 2
+    own, far = both[:size], both[size:]
+    groups = [(own, 0), (far, 2)]
+    if far_first:
+        got = yield [swap(far, "wa", 2)]
+        own = plus(own, got[0])
+        groups = [(own, 0)]
+    quarter = size // 4
+    cut = lambda a, t: lax.dynamic_slice_in_dim(a, (place ^ t) * quarter, quarter, 0)
+    got = yield [
+        swap_both(cut(a, t), t, bit) for a, bit in groups for t in range(4) if bit or t
+    ]
+    terms = [a.astype(F32) for a in [cut(own, 0)] + list(got)]
+    value = terms[0] + terms[1] + terms[2] + terms[3]
+    if not far_first:
+        value = value + (terms[4] + terms[5] + terms[6] + terms[7])
+    value = value.astype(BF)
+    for bit in bits_of("ctx")[2:]:
+        got = yield [swap(value, "ctx", bit)]
+        value = plus(value, got[0])
+    got = yield [swap(value, "ctx", t) for t in range(1, 4)]
+    quarters = jnp.stack([value] + list(got))
+    rows = [lax.dynamic_index_in_dim(quarters, place ^ t, 0, keepdims=False) for t in range(4)]
+    return jnp.concatenate(rows, 0).astype(F32)
+
+
+class Chains:
+    def __init__(self):
+        self.running, self.flying, self.results = {}, {}, {}
+
+    def start(self, name, steps):
+        self.running[name] = steps
+        self.flying[name] = next(steps)
+
+    def step(self, names, *values):
+        names = [name for name in names if name in self.running]
+        flying, values = tie([self.flying[name] for name in names], values)
+        for name, got in zip(names, flying, strict=True):
+            try:
+                self.flying[name] = self.running[name].send(got)
+            except StopIteration as end:
+                self.results[name] = end.value
+                del self.running[name]
+        return values
 
 
 def neighbours(value):
@@ -634,19 +690,15 @@
     n = lax.axis_size("wa")
     context_rank = lax.axis_index("ctx")
     seq_len = block * lax.axis_size("ctx")
+    place = context_rank & 3
     info = jnp.stack(
         [
             lax.axis_index("wa").astype(jnp.int32),
             context_rank.astype(jnp.int32),
             jnp.int32(seq_len),
+            place.astype(jnp.int32),
         ]
     )
-    left, right = neighbours(layer_input)
-    qkv_parts = gather_parts(qkv_proj.T)
-    out_parts = gather_parts(out_proj)
-    in_parts = gather_parts(in_proj.T)
-    down_parts = gather_parts(down_proj)
-
     frequencies = jnp.power(10000.0, -jnp.arange(0, HEAD, 2, dtype=F32) / HEAD)
     places = context_rank * block - HALF + jnp.arange(block + 2 * HALF, dtype=jnp.int32)
     angles = places.astype(F32)[:, None] * frequencies[None, :]
@@ -662,34 +714,67 @@
     head_of = jnp.arange(width, dtype=jnp.int32)[:, None] // HEAD
     ind = (lane == head_of + 64).astype(BF)
 
-    q, k, v, attended, soft, lse, normed1 = attend(
-        info, layer_input, left, right, attention_gain[None], tables, qkv_parts
-    )
+    quarter = down_proj.shape[0]
+    far = lambda value: swap(value, "wa", 2)
+    near = lambda value: swap(value, "wa", 1)
+    left, right = neighbours(layer_input)
+    qkv_own = qkv_proj.T
+    qkv_far, qkv_near = far(qkv_own), near(qkv_own)
+    rest_own = jnp.concatenate([in_proj.T, down_proj, out_proj], 0)
+    qkv_far, qkv_near, left, right, rest_own, tables, own_tables, ind, info = tie(
+        qkv_far, qkv_near, left, right, rest_own, tables, own_tables, ind, info
+    )
+    qkv_both = near(qkv_far)
+    rest_far, rest_near = far(rest_own), near(rest_own)
+    qkv_parts = [qkv_own, qkv_near, qkv_far, qkv_both]
+
+    gain1 = attention_gain[None]
+    made = attend(info, layer_input, left, right, gain1, tables, qkv_parts)
+    made, rest_near, rest_far = tie(made, rest_near, rest_far)
+    q, k, v, attended, soft, lse, normed1, qkv_weight = made
+    rest_parts = [rest_own, rest_near, rest_far, near(rest_far)]
     output, normed2, mixed, inner_grad, hidden_grad, branch, dom, feed_gain_grad = feed(
-        info,
-        layer_input,
-        attended,
-        cotangent,
-        lse,
-        feed_gain[None],
-        ind,
-        out_parts,
-        in_parts,
-        down_parts,
+        info, layer_input, attended, cotangent, lse, feed_gain[None], ind, rest_parts
     )
     left_grad, right_grad = neighbours(dom)
     flat = lambda a: a.reshape(rows, a.shape[-1])
-    in_grad = reduce_parts(weight_grad(info, flat(inner_grad), flat(normed2), n))
-    down_grad = reduce_parts(weight_grad(info, flat(mixed), flat(cotangent), n))
-    out_grad = reduce_parts(weight_grad(info, flat(attended), flat(branch), n))
-    projected_grad = attend_back(q, k, v, soft, dom, left_grad, right_grad, own_tables)
-    qkv_grad = reduce_parts(weight_grad(info, flat(projected_grad), flat(normed1), n))
-    input_grad, attention_gain_grad = input_back(
-        info, projected_grad, layer_input, attention_gain[None], hidden_grad, qkv_parts
-    )
-    gains = sum_all(
-        jnp.concatenate([attention_gain_grad, feed_gain_grad], 0).reshape(-1, LANES)
-    ).reshape(2, width)
+    chains = Chains()
+    in_parts = weight_grad(info, [(flat(inner_grad), flat(normed2))], n)
+    in_parts, mixed, branch, left_grad = tie(in_parts, mixed, branch, left_grad)
+    chains.start("in", reduce_steps(*in_parts, True))
+    other_parts = weight_grad(
+        info, [(flat(mixed), flat(cotangent)), (flat(attended), flat(branch))], n
+    )
+    other_parts, q, right_grad = chains.step(["in"], other_parts, q, right_grad)
+    chains.start("other", reduce_steps(*other_parts, True))
+    (q,) = chains.step(["other"], q)
+    half_seqs = seqs // 2
+    back = attend_back(
+        q, k, v, soft, dom, left_grad, right_grad, own_tables, 0, half_seqs, ()
+    )
+    back, q = chains.step(["in"], back, q)
+    back = attend_back(
+        q, k, v, soft, dom, left_grad, right_grad, own_tables, half_seqs, seqs - half_seqs, (back,)
+    )
+    (back,) = chains.step(["in", "other"], back)
+    qkv_back = weight_grad(
+        info, [(flat(back), flat(normed1))], n, (qkv_weight, gain1, feed_gain_grad)
+    )
+    qkv_back, back = chains.step(["in", "other"], qkv_back, back)
+    chains.start("qkv", reduce_steps(*qkv_back, False))
+    made = input_back(back, layer_input, gain1, hidden_grad, qkv_weight, 0, half_seqs, ())
+    made, back = chains.step(["in", "other", "qkv"], made, back)
+    input_grad = input_back(
+        back, layer_input, gain1, hidden_grad, qkv_weight, half_seqs, seqs - half_seqs, (made,)
+    )
+    (input_grad,) = chains.step(["in", "other"], input_grad)
+    while chains.running:
+        chains.step(list(chains.running))
+    qkv_grad, in_grad, other_grad = (chains.results[name] for name in ("qkv", "in", "other"))
+    qkv_rows = qkv_proj.shape[1]
+    gains = qkv_grad[qkv_rows : qkv_rows + 2]
+    qkv_grad = qkv_grad[:qkv_rows]
+    down_grad, out_grad = other_grad[:quarter], other_grad[quarter:]
     return (
         output,
         input_grad,

time: 342 us -> 287 us (0.84)
  waiting for transfers between devices: 135 us -> 64.6 us
  other arithmetic: 12.1 us -> 22 us
  Pallas kernels: 131 us -> 137 us
  starting transfers between devices: 54.7 us -> 49.1 us
  local copies, waits for them, and re-layouts: 7.04 us -> 12.5 us
    ppermute x49 -> x23, waiting for transfers between devices: 120 us -> 38.7 us  [swap(): return lax.ppermute(value, axis, [(i, i ^ bit) for i in range(count)])]
    ppermute x49 -> x23, starting transfers between devices: 42.7 us -> 21.3 us  [swap(): return lax.ppermute(value, axis, [(i, i ^ bit) for i in range(count)])]
    ppermute x0 -> x13, starting transfers between devices: none -> 16.3 us  [swap_both(): lax.ppermute(value, ('ctx', 'wa'), [(i, i ^ mask) for i in range(every)])]
    ppermute x0 -> x13, waiting for transfers between devices: none -> 11.9 us  [swap_both(): lax.ppermute(value, ('ctx', 'wa'), [(i, i ^ mask) for i in range(every)])]
    convert_element_type x20 -> x8, other arithmetic: 2.25 us -> 8.37 us  [plus(): return (a.astype(F32) + b.astype(F32)).astype(BF)]
    pallas_call x8 -> x9, Pallas kernels: 131 us -> 137 us  [the longest x2 33.8 us: attend_back(): pl.pallas_call(attend_back_kernel, grid=(count,), in_specs=[seq(span, wid...]
  transfers between devices with their start and end apart: 53 -> 40, of which waited for: 21 -> 18; matrix products, arithmetic and copies ran while one was open for 5% -> 9% of each run, Pallas kernels for 27% -> 36%
where the time goes in v2:
time: 287 us; the launch traced here: 286 us
  Pallas kernels  137 us (48%)
  waiting for transfers between devices  64.6 us (23%)
  starting transfers between devices  49.1 us (17%)
  other arithmetic  22 us (8%)
  local copies, waits for them, and re-layouts  12.5 us (4%)
    ppermute x23, waiting for transfers between devices, swap(): return lax.ppermute(value, axis, [(i, i ^ bit) for i in range(count)])  38.7 us
    pallas_call x2, Pallas kernels, attend_back(): pl.pallas_call(attend_back_kernel, grid=(count,), in_specs=[seq(span, wid...  33.8 us
    pallas_call x1, Pallas kernels, feed(): pl.pallas_call(functools.partial(feed_kernel, hidden), grid_spec=pltpu.Pr...  32.8 us
    pallas_call x3, Pallas kernels, weight_grad(): pl.pallas_call(functools.partial(weight_grad_kernel, steps, n, bool(gains...  30.3 us
    pallas_call x1, Pallas kernels, attend(): pl.pallas_call(attend_kernel, grid_spec=pltpu.PrefetchScalarGridSpec(num_...  26.8 us
    ppermute x23, starting transfers between devices, swap(): return lax.ppermute(value, axis, [(i, i ^ bit) for i in range(count)])  21.3 us
    ppermute x13, starting transfers between devices, swap_both(): lax.ppermute(value, ('ctx', 'wa'), [(i, i ^ mask) for i in range(every)])  16.3 us
    pallas_call x2, Pallas kernels, input_back(): pl.pallas_call(input_kernel, grid=(count,), in_specs=[seq(block, 3 * widt...  12.9 us
  transfers between devices with their start and end apart: 40, of which 18 were waited for; matrix products, arithmetic and copies ran while one was open for 9% of the time, Pallas kernels for 36%

profile of v2, /device:TPU:0, one launch (start us, length us, event | category | flops | bytes accessed | tf_op | source)
XLA Modules:
  0.0 285.9 jit_solution(6751164622061689798)
XLA Ops:
  0.6 3.0 %collective-permute-start = (bf16[576,768]{1,0:T(8,128)(2,1)}, bf16[576,768]{1,0:T(8,128)(2,1)}, u32[]{:S(2)}, u32[]{:S(2)}) collective-permute-start(bf16[576,768]{1,0:T(8,128)(2,1)} %bitcast.65), channel_id=1, source_target_pairs={{0,2},{1,3},{2,0},{3,1},{4,6},{5,7},{6,4},{7,5},{8,10},{9,11},{10,... | collective-permute-start | bytes 2654216 | tf_op jit(solution)/shard_map/ppermute | solution.py:603
  5.6 4.3 %collective-permute-start.2 = (bf16[4,64,768]{2,1,0:T(8,128)(2,1)}, bf16[4,64,768]{2,1,0:T(8,128)(2,1)}, u32[]{:S(2)}, u32[]{:S(2)}) collective-permute-start(bf16[4,64,768]{2,1,0:T(8,128)(2,1)} %get-tuple-element.201), channel_id=1, source_target_pairs={{0,4},{4,8},{8,12},{12,16},{16,20},{20,24},{24,28},{1,5},{5,9},{9,... | collective-permute-start | bytes 1179656 | tf_op jit(solution)/shard_map/ppermute | solution.py:679
  17.2 9.7 %collective-permute-done.2.left_ref = bf16[4,64,768]{2,1,0:T(8,128)(2,1)} collective-permute-done((bf16[4,64,768]{2,1,0:T(8,128)(2,1)}, bf16[4,64,768]{2,1,0:T(8,128)(2,1)}, u32[]{:S(2)}, u32[]{:S(2)}) %collective-permute-start.2) | collective-permute-done | bytes 393248 | tf_op jit(solution)/shard_map/ppermute | solution.py:679
  28.3 3.5 %collective-permute-done.4.rest_3_ = bf16[576,768]{1,0:T(8,128)(2,1)} collective-permute-done((bf16[576,768]{1,0:T(8,128)(2,1)}, bf16[576,768]{1,0:T(8,128)(2,1)}, u32[]{:S(2)}, u32[]{:S(2)}) %collective-permute-start.4) | collective-permute-done | bytes 884768 | tf_op jit(solution)/shard_map/ppermute | solution.py:603
  31.9 26.8 %attend.1 = (bf16[4,384,768]{2,1,0:T(8,128)(2,1)}, bf16[4,384,768]{2,1,0:T(8,128)(2,1)}, bf16[4,384,768]{2,1,0:T(8,128)(2,1)}, bf16[4,256,768]{2,1,0:T(8,128)(2,...) custom-call(s32[4]{0:T(128)} %pad_add_fusion.info, ...), custom_call_target="tpu_custom_call" | custom-call | flops 7247757312 | bytes 30000000 | tf_op jit(solution)/shard_map/attend/pallas_call | solution.py:165
  58.7 6.3 %collective-permute-done.6.rest_2_ = bf16[1056,768]{1,0:T(8,128)(2,1)} collective-permute-done((bf16[1056,768]{1,0:T(8,128)(2,1)S(1)}, bf16[1056,768]{1,0:T(8,128)(2,1)}, u32[]{:S(2)}, u32[]{:S(2)}) %collective-permute-start.6) | collective-permute-done | bytes 1622048 | tf_op jit(solution)/shard_map/ppermute | solution.py:603
  65.5 3.1 %collective-permute-done.7.rest_3_ = bf16[1056,768]{1,0:T(8,128)(2,1)S(1)} collective-permute-done((bf16[1056,768]{1,0:T(8,128)(2,1)}, bf16[1056,768]{1,0:T(8,128)(2,1)S(1)}, u32[]{:S(2)}, u32[]{:S(2)}) %collective-permute-start.7) | collective-permute-done | bytes 1622048 | tf_op jit(solution)/shard_map/ppermute | solution.py:603
  69.8 32.8 %feed.1 = (bf16[4,256,768]{2,1,0:T(8,128)(2,1)}, bf16[4,256,768]{2,1,0:T(8,128)(2,1)}, bf16[4,256,1152]{2,1,0:T(8,128)(2,1)}, bf16[4,256,2304]{2,1,0:T(8,128)(2,...) custom-call(s32[4]{0:T(128)} %pad_add_fusion.info, ...), custom_call_target="tpu_custom_call" | custom-call | flops 13287555072 | bytes 30000000 | tf_op jit(solution)/shard_map/feed/pallas_call | solution.py:298
  103.8 4.6 %collective-permute-start.8 = (bf16[4,64,896]{2,1,0:T(8,128)(2,1)S(1)}, bf16[4,64,896]{2,1,0:T(8,128)(2,1)S(1)}, u32[]{:S(2)}, u32[]{:S(2)}) collective-permute-start(bf16[4,64,896]{2,1,0:T(8,128)(2,1)S(1)} %get-tuple-element.199), channel_id=1, source_target_pairs={{0,4},{4,8},{8,12},{12,16},{16,20},{20,24},{24,28},{1,5},{5,9},{9,... | collective-permute-start | bytes 1376264 | tf_op jit(solution)/shard_map/ppermute | solution.py:679
  108.4 9.9 %weight_grad.3 = (bf16[1152,768]{1,0:T(8,128)(2,1)}, bf16[1152,768]{1,0:T(8,128)(2,1)}) custom-call(s32[4]{0:T(128)} %pad_add_fusion.info, bf16[1024,2304]{1,0:T(8,128)(2,1)} %bitcast.68, bf16[1024,768]{1,0:T(8,128)(2,1)} %bitcast.73), custom_call_target="tpu_custom_call" | custom-call | flops 3623878656 | bytes 9830400 | tf_op jit(solution)/shard_map/weight_grad/pallas_call | solution.py:544
  119.8 9.7 %weight_grad.4 = (bf16[960,768]{1,0:T(8,128)(2,1)}, bf16[960,768]{1,0:T(8,128)(2,1)}) custom-call(s32[4]{0:T(128)} %pad_add_fusion.info, bf16[1024,1152]{1,0:T(8,128)(2,1)} %bitcast.69, bf16[1024,768]{1,0:T(8,128)(2,1)} %bitcast.64, bf16[1024,768]{1,0:T(8,128)(2,1)} %bitcast.71, bf16[1024,768]{1,0:T(8,128)(2,1)} %bitcast.72), custom_call_target="tpu_custom_call" | custom-call | flops 3019898880 | bytes 8454144 | tf_op jit(solution)/shard_map/weight_grad/pallas_call | solution.py:544
  129.5 4.4 %collective-permute-done.10.right_ref = bf16[4,64,896]{2,1,0:T(8,128)(2,1)S(1)} collective-permute-done((bf16[4,64,896]{2,1,0:T(8,128)(2,1)S(1)}, bf16[4,64,896]{2,1,0:T(8,128)(2,1)S(1)}, u32[]{:S(2)}, u32[]{:S(2)}) %collective-permute-start.10) | collective-permute-done | bytes 458784 | tf_op jit(solution)/shard_map/ppermute | solution.py:680
  142.7 16.9 %attend_back.2.rest_0_ = bf16[4,256,2304]{2,1,0:T(8,128)(2,1)} custom-call(bf16[4,384,768]{2,1,0:T(8,128)(2,1)} %get-tuple-element.153.q_ref, bf16[4,384,768]{2,1,0:T(8,128)(2,1)} %get-tuple-element.144.k_ref, bf16[4,384,768]{2,1,0:T(8,128)(2,1)} %get-tuple-element.145.v_ref, bf16[4,6,2,256,256]{4,3,2,1,0:T(8,128)(2,1)} %get-tuple-element.146.p_ref, ...), custom_call_target="tpu_custom_call" | custom-call | flops 1811939328 | bytes 14000000 | tf_op jit(solution)/shard_map/attend_back/pallas_call | solution.py:437
  162.7 3.3 %collective-permute-start.13 = (bf16[144,768]{1,0:T(8,128)(2,1)S(1)}, bf16[144,768]{1,0:T(8,128)(2,1)S(1)}, u32[]{:S(2)}, u32[]{:S(2)}) collective-permute-start(bf16[144,768]{1,0:T(8,128)(2,1)S(1)} %get-tuple-element.219), channel_id=1, source_target_pairs={{0,4},{1,5},{2,6},{3,7},{4,0},{5,1},{6,2},{7,3},{8,12},{9,13},{10,... | collective-permute-start | bytes 663560 | tf_op jit(solution)/shard_map/ppermute | solution.py:623
  167.8 16.9 %attend_back.3.grad_ref = bf16[4,256,2304]{2,1,0:T(8,128)(2,1)} custom-call(bf16[4,384,768]{2,1,0:T(8,128)(2,1)} %get-tuple-element.153.q_ref, bf16[4,384,768]{2,1,0:T(8,128)(2,1)} %get-tuple-element.144.k_ref, bf16[4,384,768]{2,1,0:T(8,128)(2,1)} %get-tuple-element.145.v_ref, ...), custom_call_target="tpu_custom_call", output_to_operand_aliasing={{}: (10, {})} | custom-call | flops 1811939328 | bytes 14000000 | tf_op jit(solution)/shard_map/attend_back/pallas_call | solution.py:437
  190.7 3.0 %collective-permute-start.17 = (bf16[144,768]{1,0:T(8,128)(2,1)S(1)}, bf16[144,768]{1,0:T(8,128)(2,1)S(1)}, u32[]{:S(2)}, u32[]{:S(2)}) collective-permute-start(bf16[144,768]{1,0:T(8,128)(2,1)S(1)} %add_convert_fusion.8), channel_id=1, source_target_pairs={{0,16},{4,20},{8,24},{12,28},{16,0},{20,4},{24,8},{28,12},{1,17},{... | collective-permute-start | bytes 663560 | tf_op jit(solution)/shard_map/ppermute | solution.py:603
  193.7 10.7 %weight_grad.5 = (bf16[1216,768]{1,0:T(8,128)(2,1)}, bf16[1216,768]{1,0:T(8,128)(2,1)}) custom-call(s32[4]{0:T(128)} %pad_add_fusion.info, bf16[1024,2304]{1,0:T(8,128)(2,1)} %bitcast.53, bf16[1024,768]{1,0:T(8,128)(2,1)} %bitcast.70, bf16[2304,768]{1,0:T(8,128)(2,1)} %get-tuple-element.161.refs_2_.weight_ref, f32[1,768]{1,0:T(1,128)} %broadcast_in_dim.14.gain_ref.refs_3_, ...), custom_call_target="tpu_custom_call" | custom-call | flops 3623878656 | bytes 9830400 | tf_op jit(solution)/shard_map/weight_grad/pallas_call | solution.py:544
  210.6 6.5 %input_back.2.rest_0_ = f32[4,256,768]{2,1,0:T(8,128)} custom-call(bf16[4,256,2304]{2,1,0:T(8,128)(2,1)} %attend_back.3.grad_ref, bf16[4,256,768]{2,1,0:T(8,128)(2,1)} %x_ref.7, f32[1,768]{1,0:T(1,128)} %broadcast_in_dim.14.gain_ref.refs_3_, f32[4,256,768]{2,1,0:T(8,128)} %get-tuple-element.171.hidden_ref, ...), custom_call_target="tpu_custom_call" | custom-call | flops 1811939328 | bytes 8000000 | tf_op jit(solution)/shard_map/input_back/pallas_call | solution.py:581
  217.1 3.9 %collective-permute-done.24 = bf16[120,768]{1,0:T(8,128)(2,1)} collective-permute-done((bf16[120,768]{1,0:T(8,128)(2,1)}, bf16[120,768]{1,0:T(8,128)(2,1)}, u32[]{:S(2)}, u32[]{:S(2)}) %collective-permute-start.24) | collective-permute-done | bytes 184352 | tf_op jit(solution)/shard_map/ppermute | solution.py:603
  238.3 8.6 %collective-permute-done.32 = bf16[152,768]{1,0:T(8,128)(2,1)S(1)} collective-permute-done((bf16[152,768]{1,0:T(8,128)(2,1)S(1)}, bf16[152,768]{1,0:T(8,128)(2,1)S(1)}, u32[]{:S(2)}, u32[]{:S(2)}) %collective-permute-start.32) | collective-permute-done | bytes 233504 | tf_op jit(solution)/shard_map/ppermute | solution.py:623
  247.2 3.1 %collective-permute-done.33 = bf16[152,768]{1,0:T(8,128)(2,1)S(1)} collective-permute-done((bf16[152,768]{1,0:T(8,128)(2,1)S(1)}, bf16[152,768]{1,0:T(8,128)(2,1)S(1)}, u32[]{:S(2)}, u32[]{:S(2)}) %collective-permute-start.33) | collective-permute-done | bytes 233504 | tf_op jit(solution)/shard_map/ppermute | solution.py:623
  252.1 6.4 %input_back.3 = f32[4,256,768]{2,1,0:T(8,128)} custom-call(bf16[4,256,2304]{2,1,0:T(8,128)(2,1)} %attend_back.3.grad_ref, bf16[4,256,768]{2,1,0:T(8,128)(2,1)} %x_ref.7, f32[1,768]{1,0:T(1,128)} %broadcast_in_dim.14.gain_ref.refs_3_, f32[4,256,768]{2,1,0:T(8,128)} %get-tuple-element.171.hidden_ref, ...), custom_call_target="tpu_custom_call", output_to_operand_aliasing={{}: (5, {})} | custom-call | flops 1811939328 | bytes 8000000 | tf_op jit(solution)/shard_map/input_back/pallas_call | solution.py:581
  261.1 9.3 %collective-permute-done.36 = bf16[152,768]{1,0:T(8,128)(2,1)S(1)} collective-permute-done((bf16[152,768]{1,0:T(8,128)(2,1)S(1)}, bf16[152,768]{1,0:T(8,128)(2,1)S(1)}, u32[]{:S(2)}, u32[]{:S(2)}) %collective-permute-start.36) | collective-permute-done | bytes 233504 | tf_op jit(solution)/shard_map/ppermute | solution.py:603
  280.0 3.7 %collective-permute-done.39 = bf16[152,768]{1,0:T(8,128)(2,1)S(1)} collective-permute-done((bf16[152,768]{1,0:T(8,128)(2,1)S(1)}, bf16[152,768]{1,0:T(8,128)(2,1)S(1)}, u32[]{:S(2)}, u32[]{:S(2)}) %collective-permute-start.39) | collective-permute-done | bytes 233504 | tf_op jit(solution)/shard_map/ppermute | solution.py:603
  (158 shorter events, 74.4 us)
Async XLA Ops:
  0.6 26.3 %collective-permute-start = (bf16[576,768]{1,0:T(8,128)(2,1)}, bf16[576,768]{1,0:T(8,128)(2,1)}, u32[]{:S(2)}, u32[]{:S(2)}) collective-permute-start(bf16[576,768]{1,0:T(8,128)(2,1)} %bitcast.65), channel_id=1, source_target_pairs={{0,2},{1,3},{2,0},{3,1},{4,6},{5,7},{6,4},{7,5},{8,10},{9,11},{10,... | collective-permute-start | bytes 2654216 | tf_op jit(solution)/shard_map/ppermute | solution.py:603
  3.7 23.3 %collective-permute-start.1 = (bf16[576,768]{1,0:T(8,128)(2,1)}, bf16[576,768]{1,0:T(8,128)(2,1)}, u32[]{:S(2)}, u32[]{:S(2)}) collective-permute-start(bf16[576,768]{1,0:T(8,128)(2,1)} %bitcast.66), channel_id=1, source_target_pairs={{0,1},{1,0},{2,3},{3,2},{4,5},{5,4},{6,7},{7,6},{8,9},{9,8},{10,11... | collective-permute-start | bytes 2654216 | tf_op jit(solution)/shard_map/ppermute | solution.py:603
  5.6 21.3 %collective-permute-start.2 = (bf16[4,64,768]{2,1,0:T(8,128)(2,1)}, bf16[4,64,768]{2,1,0:T(8,128)(2,1)}, u32[]{:S(2)}, u32[]{:S(2)}) collective-permute-start(bf16[4,64,768]{2,1,0:T(8,128)(2,1)} %get-tuple-element.201), channel_id=1, source_target_pairs={{0,4},{4,8},{8,12},{12,16},{16,20},{20,24},{24,28},{1,5},{5,9},{9,... | collective-permute-start | bytes 1179656 | tf_op jit(solution)/shard_map/ppermute | solution.py:679
  9.9 17.0 %collective-permute-start.3 = (bf16[4,64,768]{2,1,0:T(8,128)(2,1)S(1)}, bf16[4,64,768]{2,1,0:T(8,128)(2,1)}, u32[]{:S(2)}, u32[]{:S(2)}) collective-permute-start(bf16[4,64,768]{2,1,0:T(8,128)(2,1)S(1)} %get-tuple-element.200), channel_id=1, source_target_pairs={{4,0},{8,4},{12,8},{16,12},{20,16},{24,20},{28,24},{5,1},{9,5},{13... | collective-permute-start | bytes 1179656 | tf_op jit(solution)/shard_map/ppermute | solution.py:680
  26.9 31.8 %collective-permute-start.5 = (bf16[1056,768]{1,0:T(8,128)(2,1)S(1)}, bf16[1056,768]{1,0:T(8,128)(2,1)S(1)}, u32[]{:S(2)}, u32[]{:S(2)}) collective-permute-start(bf16[1056,768]{1,0:T(8,128)(2,1)S(1)} %pad_maximum_fusion.rest_0_), channel_id=1, source_target_pairs={{0,1},{1,0},{2,3},{3,2},{4,5},{5,4},{6,7},{7,6},{8,9},{9,8},{10,11... | collective-permute-start | bytes 4866056 | tf_op jit(solution)/shard_map/ppermute | solution.py:603
  27.0 38.0 %collective-permute-start.6 = (bf16[1056,768]{1,0:T(8,128)(2,1)S(1)}, bf16[1056,768]{1,0:T(8,128)(2,1)}, u32[]{:S(2)}, u32[]{:S(2)}) collective-permute-start(bf16[1056,768]{1,0:T(8,128)(2,1)S(1)} %pad_maximum_fusion.rest_0_), channel_id=1, source_target_pairs={{0,2},{1,3},{2,0},{3,1},{4,6},{5,7},{6,4},{7,5},{8,10},{9,11},{10,... | collective-permute-start | bytes 4866056 | tf_op jit(solution)/shard_map/ppermute | solution.py:603
  118.4 15.5 %collective-permute-start.9 = (bf16[1152,768]{1,0:T(8,128)(2,1)}, bf16[1152,768]{1,0:T(8,128)(2,1)}, u32[]{:S(2)}, u32[]{:S(2)}) collective-permute-start(bf16[1152,768]{1,0:T(8,128)(2,1)} %get-tuple-element.131), channel_id=1, source_target_pairs={{0,1},{1,0},{2,3},{3,2},{4,5},{5,4},{6,7},{7,6},{8,9},{9,8},{10,11... | collective-permute-start | bytes 5308424 | tf_op jit(solution)/shard_map/ppermute | solution.py:603
  118.5 15.4 %collective-permute-start.10 = (bf16[4,64,896]{2,1,0:T(8,128)(2,1)S(1)}, bf16[4,64,896]{2,1,0:T(8,128)(2,1)S(1)}, u32[]{:S(2)}, u32[]{:S(2)}) collective-permute-start(bf16[4,64,896]{2,1,0:T(8,128)(2,1)S(1)} %get-tuple-element.198), channel_id=1, source_target_pairs={{4,0},{8,4},{12,8},{16,12},{20,16},{24,20},{28,24},{5,1},{9,5},{13... | collective-permute-start | bytes 1376264 | tf_op jit(solution)/shard_map/ppermute | solution.py:680
  137.5 22.8 %collective-permute-start.12 = (bf16[576,768]{1,0:T(8,128)(2,1)}, bf16[576,768]{1,0:T(8,128)(2,1)}, u32[]{:S(2)}, u32[]{:S(2)}) collective-permute-start(bf16[576,768]{1,0:T(8,128)(2,1)} %slice.80), channel_id=1, source_target_pairs={{0,2},{1,3},{2,0},{3,1},{4,6},{5,7},{6,4},{7,5},{8,10},{9,11},{10,... | collective-permute-start | bytes 2654216 | tf_op jit(solution)/shard_map/ppermute | solution.py:603
  141.4 43.3 %collective-permute-start.16 = (bf16[480,768]{1,0:T(8,128)(2,1)}, bf16[480,768]{1,0:T(8,128)(2,1)}, u32[]{:S(2)}, u32[]{:S(2)}) collective-permute-start(bf16[480,768]{1,0:T(8,128)(2,1)} %slice.81), channel_id=1, source_target_pairs={{0,2},{1,3},{2,0},{3,1},{4,6},{5,7},{6,4},{7,5},{8,10},{9,11},{10,... | collective-permute-start | bytes 2211848 | tf_op jit(solution)/shard_map/ppermute | solution.py:603
  162.7 22.0 %collective-permute-start.13 = (bf16[144,768]{1,0:T(8,128)(2,1)S(1)}, bf16[144,768]{1,0:T(8,128)(2,1)S(1)}, u32[]{:S(2)}, u32[]{:S(2)}) collective-permute-start(bf16[144,768]{1,0:T(8,128)(2,1)S(1)} %get-tuple-element.219), channel_id=1, source_target_pairs={{0,4},{1,5},{2,6},{3,7},{4,0},{5,1},{6,2},{7,3},{8,12},{9,13},{10,... | collective-permute-start | bytes 663560 | tf_op jit(solution)/shard_map/ppermute | solution.py:623
  166.0 18.7 %collective-permute-start.14 = (bf16[144,768]{1,0:T(8,128)(2,1)S(1)}, bf16[144,768]{1,0:T(8,128)(2,1)S(1)}, u32[]{:S(2)}, u32[]{:S(2)}) collective-permute-start(bf16[144,768]{1,0:T(8,128)(2,1)S(1)} %get-tuple-element.218), channel_id=1, source_target_pairs={{0,8},{1,9},{2,10},{3,11},{4,12},{5,13},{6,14},{7,15},{8,0},{9,1},... | collective-permute-start | bytes 663560 | tf_op jit(solution)/shard_map/ppermute | solution.py:623
  167.6 17.1 %collective-permute-start.15 = (bf16[144,768]{1,0:T(8,128)(2,1)S(1)}, bf16[144,768]{1,0:T(8,128)(2,1)S(1)}, u32[]{:S(2)}, u32[]{:S(2)}) collective-permute-start(bf16[144,768]{1,0:T(8,128)(2,1)S(1)} %get-tuple-element.217), channel_id=1, source_target_pairs={{0,12},{1,13},{2,14},{3,15},{4,8},{5,9},{6,10},{7,11},{8,4},{9,5},... | collective-permute-start | bytes 663560 | tf_op jit(solution)/shard_map/ppermute | solution.py:623
  186.0 18.3 %collective-permute-start.18 = (bf16[120,768]{1,0:T(8,128)(2,1)S(1)}, bf16[120,768]{1,0:T(8,128)(2,1)}, u32[]{:S(2)}, u32[]{:S(2)}) collective-permute-start(bf16[120,768]{1,0:T(8,128)(2,1)S(1)} %get-tuple-element.226), channel_id=1, source_target_pairs={{0,4},{1,5},{2,6},{3,7},{4,0},{5,1},{6,2},{7,3},{8,12},{9,13},{10,... | collective-permute-start | bytes 552968 | tf_op jit(solution)/shard_map/ppermute | solution.py:623
  187.8 16.6 %collective-permute-start.19 = (bf16[120,768]{1,0:T(8,128)(2,1)S(1)}, bf16[120,768]{1,0:T(8,128)(2,1)}, u32[]{:S(2)}, u32[]{:S(2)}) collective-permute-start(bf16[120,768]{1,0:T(8,128)(2,1)S(1)} %get-tuple-element.225), channel_id=1, source_target_pairs={{0,8},{1,9},{2,10},{3,11},{4,12},{5,13},{6,14},{7,15},{8,0},{9,1},... | collective-permute-start | bytes 552968 | tf_op jit(solution)/shard_map/ppermute | solution.py:623
  189.3 15.0 %collective-permute-start.20 = (bf16[120,768]{1,0:T(8,128)(2,1)S(1)}, bf16[120,768]{1,0:T(8,128)(2,1)S(1)}, u32[]{:S(2)}, u32[]{:S(2)}) collective-permute-start(bf16[120,768]{1,0:T(8,128)(2,1)S(1)} %get-tuple-element.224), channel_id=1, source_target_pairs={{0,12},{1,13},{2,14},{3,15},{4,8},{5,9},{6,10},{7,11},{8,4},{9,5},... | collective-permute-start | bytes 552968 | tf_op jit(solution)/shard_map/ppermute | solution.py:623
  205.1 17.9 %collective-permute-start.25 = (bf16[1216,768]{1,0:T(8,128)(2,1)}, bf16[1216,768]{1,0:T(8,128)(2,1)S(1)}, u32[]{:S(2)}, u32[]{:S(2)}) collective-permute-start(bf16[1216,768]{1,0:T(8,128)(2,1)} %get-tuple-element.169), channel_id=1, source_target_pairs={{0,1},{1,0},{2,3},{3,2},{4,5},{5,4},{6,7},{7,6},{8,9},{9,8},{10,11... | collective-permute-start | bytes 5603336 | tf_op jit(solution)/shard_map/ppermute | solution.py:603
  205.1 15.9 %collective-permute-start.21 = (bf16[144,768]{1,0:T(8,128)(2,1)S(1)}, bf16[144,768]{1,0:T(8,128)(2,1)}, u32[]{:S(2)}, u32[]{:S(2)}) collective-permute-start(bf16[144,768]{1,0:T(8,128)(2,1)S(1)} %add_convert_fusion.7), channel_id=1, source_target_pairs={{0,4},{4,0},{8,12},{12,8},{16,20},{20,16},{24,28},{28,24},{1,5},{5... | collective-permute-start | bytes 663560 | tf_op jit(solution)/shard_map/ppermute | solution.py:603
  206.8 16.2 %collective-permute-start.23 = (bf16[144,768]{1,0:T(8,128)(2,1)S(1)}, bf16[144,768]{1,0:T(8,128)(2,1)}, u32[]{:S(2)}, u32[]{:S(2)}) collective-permute-start(bf16[144,768]{1,0:T(8,128)(2,1)S(1)} %add_convert_fusion.7), channel_id=1, source_target_pairs={{0,12},{4,8},{8,4},{12,0},{16,28},{20,24},{24,20},{28,16},{1,13},{... | collective-permute-start | bytes 663560 | tf_op jit(solution)/shard_map/ppermute | solution.py:603
  228.3 18.6 %collective-permute-start.32 = (bf16[152,768]{1,0:T(8,128)(2,1)S(1)}, bf16[152,768]{1,0:T(8,128)(2,1)S(1)}, u32[]{:S(2)}, u32[]{:S(2)}) collective-permute-start(bf16[152,768]{1,0:T(8,128)(2,1)S(1)} %get-tuple-element.209), channel_id=1, source_target_pairs={{0,2},{1,3},{2,0},{3,1},{4,6},{5,7},{6,4},{7,5},{8,10},{9,11},{10,... | collective-permute-start | bytes 700424 | tf_op jit(solution)/shard_map/ppermute | solution.py:623
  228.9 21.4 %collective-permute-start.33 = (bf16[152,768]{1,0:T(8,128)(2,1)S(1)}, bf16[152,768]{1,0:T(8,128)(2,1)S(1)}, u32[]{:S(2)}, u32[]{:S(2)}) collective-permute-start(bf16[152,768]{1,0:T(8,128)(2,1)S(1)} %get-tuple-element.208), channel_id=1, source_target_pairs={{0,6},{1,7},{2,4},{3,5},{4,2},{5,3},{6,0},{7,1},{8,14},{9,15},{10,... | collective-permute-start | bytes 700424 | tf_op jit(solution)/shard_map/ppermute | solution.py:623
  232.6 25.9 %collective-permute-start.34 = (bf16[152,768]{1,0:T(8,128)(2,1)S(1)}, bf16[152,768]{1,0:T(8,128)(2,1)S(1)}, u32[]{:S(2)}, u32[]{:S(2)}) collective-permute-start(bf16[152,768]{1,0:T(8,128)(2,1)S(1)} %get-tuple-element.207), channel_id=1, source_target_pairs={{0,10},{1,11},{2,8},{3,9},{4,14},{5,15},{6,12},{7,13},{8,2},{9,3},... | collective-permute-start | bytes 700424 | tf_op jit(solution)/shard_map/ppermute | solution.py:623
  233.0 25.6 %collective-permute-start.35 = (bf16[152,768]{1,0:T(8,128)(2,1)S(1)}, bf16[152,768]{1,0:T(8,128)(2,1)S(1)}, u32[]{:S(2)}, u32[]{:S(2)}) collective-permute-start(bf16[152,768]{1,0:T(8,128)(2,1)S(1)} %get-tuple-element.206), channel_id=1, source_target_pairs={{0,14},{1,15},{2,12},{3,13},{4,10},{5,11},{6,8},{7,9},{8,6},{9,7},... | collective-permute-start | bytes 700424 | tf_op jit(solution)/shard_map/ppermute | solution.py:623
  237.0 21.5 %collective-permute-start.29 = (bf16[152,768]{1,0:T(8,128)(2,1)S(1)}, bf16[152,768]{1,0:T(8,128)(2,1)S(1)}, u32[]{:S(2)}, u32[]{:S(2)}) collective-permute-start(bf16[152,768]{1,0:T(8,128)(2,1)S(1)} %get-tuple-element.212), channel_id=1, source_target_pairs={{0,4},{1,5},{2,6},{3,7},{4,0},{5,1},{6,2},{7,3},{8,12},{9,13},{10,... | collective-permute-start | bytes 700424 | tf_op jit(solution)/shard_map/ppermute | solution.py:623
  (40 other events, 398.6 us)
